TPU v7x, 32 devices: a whole 2x2x4 slice. The times are simulated.
32 devices in a mesh: row: 16 (over z, y, x), col: 2 (over core).
Axes of the slice: x: 2, y: 2, z: 4, core: 2. Of those that a mesh axis runs over, the one named last changes fastest.
Arguments:
- panel: bfloat16 [65536, 256], P('row'), may hold values from -400 to 400, as said below
- slab: bfloat16 [65536, 1024], P('row', 'col'), may hold values from -300 to 300
Outputs:
- factor: float32 [256, 256], P(None, 'col')
- coupling: float32 [256, 1024], P(None, 'col')
- remainder: bfloat16 [65536, 1024], P('row', 'col')
Inputs may be any that keep to these rules, and one draw needn't show every extreme that they name: panel has full column rank.
All inputs are finite; a program needn't handle non-finite values.
Results may differ from a plain program's by a relative error of at most 0.015.
The roundings to bfloat16 on the way count: a program that leaves them out, or rounds other values in their place, can miss the bound.
Values sent between devices are 32-bit elements; how exact they have to be, the bound alone decides.
A program may use at most 64 MiB of HBM per device.

v0:
```python
import jax
import jax.numpy as jnp
from jax import lax
from jax.experimental import pallas as pl
from jax.experimental.pallas import tpu as pltpu

HI = lax.Precision.HIGHEST


def mm(a, b, ca=1, cb=0):
    return lax.dot_general(a, b, (((ca,), (cb,)), ((), ())), precision=HI, preferred_element_type=jnp.float32)


def eliminate(block, r_ref, w_ref):
    n = block.shape[0]
    groups = n // 8
    lane = lax.broadcasted_iota(jnp.int32, (8, n), 1)
    sub = lax.broadcasted_iota(jnp.int32, (8, n), 0)
    a = [block[8 * t : 8 * t + 8, :] for t in range(groups)]
    w = [jnp.where(lane == sub + 8 * t, 1.0, 0.0).astype(jnp.float32) for t in range(groups)]

    def group(g, carry):
        a, w = list(carry[0]), list(carry[1])
        for j in range(8):
            inv = lax.rsqrt(jnp.broadcast_to(a[0][j : j + 1, j : j + 1], (8, n)))
            arow = jnp.broadcast_to(a[0][j : j + 1, :], (8, n)) * inv
            wrow = jnp.broadcast_to(w[0][j : j + 1, :], (8, n)) * inv
            for t in range(groups):
                col = jnp.broadcast_to(a[t][:, j : j + 1], (8, n)) * inv
                if t == 0:
                    below = sub > j
                    here = sub == j
                    a[0], w[0] = (
                        jnp.where(here, arow, jnp.where(below, a[0] - col * arow, a[0])),
                        jnp.where(here, wrow, jnp.where(below, w[0] - col * wrow, w[0])),
                    )
                else:
                    a[t] = a[t] - col * arow
                    w[t] = w[t] - col * wrow
        start = pl.multiple_of(8 * g, 8)
        r = pltpu.roll(a[0], 8 * g, 1)
        r_ref[pl.ds(start, 8), :] = jnp.where(lane >= sub + 8 * g, r, 0.0)
        w_ref[pl.ds(start, 8), :] = w[0]
        zero = jnp.zeros((8, n), jnp.float32)
        a = [pltpu.roll(x, n - 8, 1) for x in a[1:]] + [zero]
        w = w[1:] + [zero]
        return tuple(a), tuple(w)

    lax.fori_loop(0, groups, group, (tuple(a), tuple(w)))


def factor_kernel(gram_ref, factor_ref, invt_ref, r_ref, w_ref):
    h = gram_ref.shape[0] // 2
    eliminate(gram_ref[:h, :h], r_ref, w_ref)
    w1 = w_ref[...]
    factor_ref[:h, :h] = r_ref[...]
    invt_ref[:h, :h] = w1
    r12 = mm(w1, gram_ref[:h, h:])
    factor_ref[:h, h:] = r12
    factor_ref[h:, :h] = jnp.zeros((h, h), jnp.float32)
    invt_ref[:h, h:] = jnp.zeros((h, h), jnp.float32)
    eliminate(gram_ref[h:, h:] - mm(r12, r12, 0, 0), r_ref, w_ref)
    w2 = w_ref[...]
    factor_ref[h:, h:] = r_ref[...]
    invt_ref[h:, h:] = w2
    invt_ref[h:, :h] = -mm(w2, mm(r12, w1, 0, 0))


def factor_and_invt(gram):
    n = gram.shape[0]
    h = n // 2
    out = jax.ShapeDtypeStruct((n, n), jnp.float32)
    return pl.pallas_call(
        factor_kernel,
        out_shape=(out, out),
        scratch_shapes=[pltpu.VMEM((h, h), jnp.float32), pltpu.VMEM((h, h), jnp.float32)],
        cost_estimate=pl.CostEstimate(flops=60_000_000, bytes_accessed=3 * n * n * 4, transcendentals=n),
        name="factor",
    )(gram)


def on_device(panel, slab):
    total_rows = panel.shape[0] * lax.axis_size("row")
    scale = 1.0 / total_rows
    contract = (((0,), (0,)), ((), ()))
    gram = lax.psum(lax.dot_general(panel, panel, contract, preferred_element_type=jnp.float32) * scale, "row")
    local_cross = lax.dot_general(panel, slab, contract, preferred_element_type=jnp.float32) * scale
    cross = lax.psum(local_cross, "row")
    factor, invt = factor_and_invt(gram)
    coupling = mm(invt, cross)
    update = mm(invt, coupling, 0, 0).astype(jnp.bfloat16)
    remainder = (slab.astype(jnp.float32) - jnp.dot(panel, update, preferred_element_type=jnp.float32)).astype(jnp.bfloat16)
    share = factor.shape[1] // lax.axis_size("col")
    factor_part = lax.dynamic_slice_in_dim(factor, lax.axis_index("col") * share, share, 1)
    return (factor_part, coupling, remainder)


def solution(mesh):
    from jax.sharding import PartitionSpec as P

    return jax.shard_map(
        on_device,
        mesh=mesh,
        in_specs=(P("row", None), P("row", "col")),
        out_specs=(P(None, "col"), P(None, "col"), P("row", "col")),
        check_vma=False,
    )
```

profile of v0, /device:TPU:0, one launch (start us, length us, event | category | flops | bytes accessed | tf_op | source)
XLA Modules:
  0.0 185.1 jit_solution(6760276120426760906)
XLA Ops:
  7.2 0.0 copy-start
  7.2 0.0 all-reduce.3.cloned.1.call-start
  7.2 1.5 copy-done
  8.8 0.0 copy-start.1
  8.8 1.4 convolution_multiply_fusion.1
  10.2 0.8 copy-done.1
  11.0 2.1 %convolution_multiply_fusion = f32[256,512]{1,0:T(8,128)} fusion(bf16[4096,256]{1,0:T(8,128)(2,1)S(1)} %copy-done, bf16[4096,512]{1,0:T(8,128)(2,1)S(1)} %copy-done.1), kind=kOutput, calls=%fused_computation.2 | convolution fusion | flops 1073872896 | bytes 6815744 | tf_op jit(solution)/shard_map/dot_general | solution.py:87
  13.1 0.0 all-reduce.3.cloned.1.call-update
  13.1 6.3 %copy.5 = bf16[4096,512]{0,1:T(8,128)(2,1)} copy(bf16[4096,512]{1,0:T(8,128)(2,1)} %param.3) | data formatting | bytes 8388608 | tf_op args[1]
  19.5 108.3 %all-reduce.3.cloned.1.call-done = (f32[256,256]{1,0:T(8,128)}, f32[256,512]{1,0:T(8,128)}) async-done(((f32[256,256]{1,0:T(8,128)}, f32[256,512]{1,0:T(8,128)}), (f32[256,256]{1,0:T(8,128)}, f32[256,512]{1,0:T(8,128)})) %all-reduce.3.cloned.1.call-update) | async-done | bytes 786448 | tf_op jit(solution)/shard_map/psum | solution.py:86
  127.8 34.4 %factor.1 = (f32[256,256]{1,0:T(8,128)}, f32[256,256]{1,0:T(8,128)}) custom-call(f32[256,256]{1,0:T(8,128)} %get-tuple-element.10.gram_ref), custom_call_target="tpu_custom_call" | custom-call | flops 60000000 | bytes 786432 | tf_op jit(solution)/shard_map/factor/pallas_call | solution.py:73
  162.1 1.7 fusion.1
  163.9 0.0 copy-start.2
  163.9 1.8 convolution_convert_fusion
  165.7 5.4 %fusion = bf16[4096,512]{0,1:T(8,128)(2,1)} fusion(bf16[4096,512]{0,1:T(8,128)(2,1)} %copy.5, bf16[256,512]{1,0:T(8,128)(2,1)S(1)} %convolution_convert_fusion, bf16[4096,256]{1,0:T(8,128)(2,1)S(1)} %copy-done), kind=kOutput, calls=%fused_computation.1 | convolution fusion | flops 1080033280 | bytes 10747904 | tf_op jit(solution)/shard_map/dot_general | solution.py:92
  171.1 0.0 copy-done.2
  171.1 0.0 copy-start.3
  171.1 6.4 %copy.6 = bf16[4096,512]{1,0:T(8,128)(2,1)} copy(bf16[4096,512]{0,1:T(8,128)(2,1)} %fusion) | data formatting | bytes 8388608
  177.6 0.0 copy-done.3
  177.6 0.7 constant_dynamic-slice_fusion
Async XLA Ops:
  7.2 1.6 copy-start
  7.2 120.6 %all-reduce.3.cloned.1.call-start = ((), (), s32[]{:S(2)}) async-start(), calls=%async_computation | async-start | bytes 1572864 | tf_op jit(solution)/shard_map/psum | solution.py:86
  8.8 2.3 %copy-start.1 = (bf16[4096,512]{1,0:T(8,128)(2,1)S(1)}, bf16[4096,512]{1,0:T(8,128)(2,1)}, u32[]{:S(2)}) copy-start(bf16[4096,512]{1,0:T(8,128)(2,1)} %param.3) | copy-start | bytes 12582916
  163.9 7.2 %copy-start.2 = (f32[256,512]{1,0:T(8,128)}, f32[256,512]{1,0:T(8,128)S(1)}, u32[]{:S(2)}) copy-start(f32[256,512]{1,0:T(8,128)S(1)} %fusion.1) | copy-start | bytes 1572868
  171.1 6.4 %copy-start.3 = (f32[256,256]{1,0:T(8,128)S(1)}, f32[256,256]{1,0:T(8,128)}, u32[]{:S(2)}) copy-start(f32[256,256]{1,0:T(8,128)} %get-tuple-element.5) | copy-start | bytes 786436
Sparse Core Ops, SparseCore 0:
  14.0 113.7 all-reduce.2
where the time goes:
time: 186 us; the launch traced here: 185 us
  waiting for transfers between devices  108 us (58%)
  Pallas kernels  34.4 us (18%)
  local copies, waits for them, and re-layouts  15.8 us (8%)
  between operations  14.1 us (8%)
  matrix products  12.4 us (7%)
    psum x1, waiting for transfers between devices, on_device(): lax.psum(lax.dot_general(panel, panel, contract, preferred_element_type=j...  108 us
    pallas_call x1, Pallas kernels, factor_and_invt(): pl.pallas_call(factor_kernel, out_shape=(out, out), scratch_shapes=[pltpu...  34.4 us
    unnamed x10, local copies, waits for them, and re-layouts  15.2 us
    dot_general x1, matrix products, on_device(): jnp.dot(panel, update, preferred_element_type=jnp.float32)  5.44 us
  transfers between devices with their start and end apart: 1, of which 1 were waited for; matrix products, arithmetic and copies ran while one was open for 3% of the time, Pallas kernels for 0%

commit v1 on v0

--- a/solution.py
+++ b/solution.py
@@ -1,3 +1,5 @@
+import functools
+
 import jax
 import jax.numpy as jnp
 from jax import lax
@@ -5,6 +7,7 @@
 from jax.experimental.pallas import tpu as pltpu
 
 HI = lax.Precision.HIGHEST
+MESH = pl.DeviceIdType.MESH
 
 
 def mm(a, b, ca=1, cb=0):
@@ -50,25 +53,25 @@
 
 
 def factor_kernel(gram_ref, factor_ref, invt_ref, r_ref, w_ref):
-    h = gram_ref.shape[0] // 2
-    eliminate(gram_ref[:h, :h], r_ref, w_ref)
+    h = gram_ref.shape[1]
+    eliminate(gram_ref[:h, :], r_ref, w_ref)
     w1 = w_ref[...]
     factor_ref[:h, :h] = r_ref[...]
     invt_ref[:h, :h] = w1
-    r12 = mm(w1, gram_ref[:h, h:])
+    r12 = mm(w1, gram_ref[h : 2 * h, :])
     factor_ref[:h, h:] = r12
     factor_ref[h:, :h] = jnp.zeros((h, h), jnp.float32)
     invt_ref[:h, h:] = jnp.zeros((h, h), jnp.float32)
-    eliminate(gram_ref[h:, h:] - mm(r12, r12, 0, 0), r_ref, w_ref)
+    eliminate(gram_ref[2 * h :, :] - mm(r12, r12, 0, 0), r_ref, w_ref)
     w2 = w_ref[...]
     factor_ref[h:, h:] = r_ref[...]
     invt_ref[h:, h:] = w2
     invt_ref[h:, :h] = -mm(w2, mm(r12, w1, 0, 0))
 
 
-def factor_and_invt(gram):
-    n = gram.shape[0]
-    h = n // 2
+def factor_and_invt(blocks):
+    h = blocks.shape[1]
+    n = 2 * h
     out = jax.ShapeDtypeStruct((n, n), jnp.float32)
     return pl.pallas_call(
         factor_kernel,
@@ -76,21 +79,267 @@
         scratch_shapes=[pltpu.VMEM((h, h), jnp.float32), pltpu.VMEM((h, h), jnp.float32)],
         cost_estimate=pl.CostEstimate(flops=60_000_000, bytes_accessed=3 * n * n * 4, transcendentals=n),
         name="factor",
-    )(gram)
+    )(blocks)
+
+
+def levels(rows):
+    inner = 1
+    while inner * inner * 4 <= rows:
+        inner *= 2
+    return inner, rows // inner
+
+
+def sums_kernel(
+    inner, outer, cols, split, scale,
+    panel_hbm, slab_hbm, gram_out, cross_out,
+    panel, slab, g_own, g_in, g_mid, g_all, x_own, x_in, x_mid, x_mid_in, x_all,
+    load_sem, g_sem, x_sem, out_sem,
+):
+    row = lax.axis_index("row")
+    col = lax.axis_index("col")
+    high, low = row // inner, row % inner
+    f32 = jnp.float32
+
+    def near(d):
+        return high * inner + (low + d) % inner
+
+    def far(d):
+        return ((high + d) % outer) * inner + low
+
+    chunks = panel.shape[0] // load_sem.shape[1]
+    steps = load_sem.shape[1]
+    loads = []
+    for t in range(steps):
+        part = pl.ds(t * chunks, chunks)
+        loads.append(pltpu.make_async_copy(panel_hbm.at[part], panel.at[part], load_sem.at[0, t]))
+    for t in range(steps):
+        part = pl.ds(t * chunks, chunks)
+        loads.append(pltpu.make_async_copy(slab_hbm.at[part], slab.at[part], load_sem.at[1, t]))
+    for copy in loads:
+        copy.start()
+
+    barrier = pltpu.get_barrier_semaphore()
+    greeted = 0
+    for d in range(inner):
+        for e in range(cols if split > 1 else 1):
+            if d or e:
+                pl.semaphore_signal(barrier, 1, device_id={"row": near(d), "col": (col + e) % cols}, device_id_type=MESH)
+                greeted += 1
+    for d in range(1, outer):
+        pl.semaphore_signal(barrier, 1, device_id={"row": far(d), "col": col}, device_id_type=MESH)
+        greeted += 1
+
+    def send(src, dst, sems, index, to_row, to_col):
+        copy = pltpu.make_async_remote_copy(
+            src_ref=src, dst_ref=dst, send_sem=sems.at[0, index], recv_sem=sems.at[1, index],
+            device_id={"row": to_row, "col": to_col}, device_id_type=MESH,
+        )
+        copy.start()
+        return copy
+
+    def tdot(a, b):
+        return lax.dot_general(a, b, (((0,), (0,)), ((), ())), preferred_element_type=f32)
+
+    h = g_own.shape[1]
+    acc = None
+    for t in range(steps):
+        loads[t].wait()
+        p = panel[t * chunks : (t + 1) * chunks, :]
+        term = tdot(p, p)
+        acc = term if acc is None else acc + term
+    acc = acc * scale
+    g_own[:h, :] = acc[:h, :h]
+    g_own[h : 2 * h, :] = acc[:h, h:]
+    g_own[2 * h :, :] = acc[h:, h:]
+
+    pl.semaphore_wait(barrier, greeted)
+
+    share = g_own.shape[0] // split
+    piece = share // inner
+    base = (col * share) if split > 1 else 0
+    g1 = []
+    for d in range(1, inner):
+        at = pl.multiple_of(base + ((low + d) % inner) * piece, 8)
+        g1.append(send(g_own.at[pl.ds(at, piece)], g_in.at[d - 1], g_sem, d - 1, near(d), col))
+    used = inner - 1
+
+    acc = None
+    for t in range(steps):
+        loads[steps + t].wait()
+        term = tdot(panel[t * chunks : (t + 1) * chunks, :], slab[t * chunks : (t + 1) * chunks, :])
+        acc = term if acc is None else acc + term
+    x_own[...] = acc * scale
+
+    xp = x_own.shape[0] // inner
+    x1 = []
+    for d in range(1, inner):
+        at = pl.multiple_of(((low + d) % inner) * xp, 8)
+        x1.append(send(x_own.at[pl.ds(at, xp)], x_in.at[d - 1], x_sem, d - 1, near(d), col))
+    xused = inner - 1
+
+    mine = pl.multiple_of(base + low * piece, 8)
+    total = g_own[pl.ds(mine, piece), :]
+    for d in range(1, inner):
+        g1[d - 1].wait()
+        total = total + g_in[d - 1]
+    g_mid[high] = total
+    g2 = []
+    for d in range(1, outer):
+        g2.append(send(g_mid.at[high], g_mid.at[high], g_sem, used + d - 1, far(d), col))
+    used += outer - 1
+    for copy in g2:
+        copy.wait()
+    total = g_mid[0]
+    for q in range(1, outer):
+        total = total + g_mid[q]
+    g_all[pl.ds(mine, piece), :] = total
+    g3 = []
+    for d in range(inner):
+        for e in range(cols if split > 1 else 1):
+            if d or e:
+                part = g_all.at[pl.ds(mine, piece)]
+                g3.append(send(part, part, g_sem, used, near(d), (col + e) % cols))
+                used += 1
+
+    at = pl.multiple_of(low * xp, 8)
+    total = x_own[pl.ds(at, xp), :]
+    for d in range(1, inner):
+        x1[d - 1].wait()
+        total = total + x_in[d - 1]
+    xq = xp // outer
+    if xq % 8 == 0:
+        x_mid[...] = total
+        x2 = []
+        for d in range(1, outer):
+            there = pl.multiple_of(((high + d) % outer) * xq, 8)
+            x2.append(send(x_mid.at[pl.ds(there, xq)], x_mid_in.at[d - 1], x_sem, xused + d - 1, far(d), col))
+        xused += outer - 1
+        here = pl.multiple_of(high * xq, 8)
+        total = x_mid[pl.ds(here, xq), :]
+        for d in range(1, outer):
+            x2[d - 1].wait()
+            total = total + x_mid_in[d - 1]
+        spot = pl.multiple_of(low * xp + high * xq, 8)
+        x_all[pl.ds(spot, xq), :] = total
+        x3 = []
+        for d in range(1, outer):
+            part = x_all.at[pl.ds(spot, xq)]
+            x3.append(send(part, part, x_sem, xused + d - 1, far(d), col))
+        xused += outer - 1
+        for copy in x3:
+            copy.wait()
+    else:
+        x_mid_in[high] = total
+        x2 = []
+        for d in range(1, outer):
+            x2.append(send(x_mid_in.at[high], x_mid_in.at[high], x_sem, xused + d - 1, far(d), col))
+        xused += outer - 1
+        for copy in x2:
+            copy.wait()
+        total = x_mid_in[0]
+        for q in range(1, outer):
+            total = total + x_mid_in[q]
+        x_all[pl.ds(at, xp), :] = total
+    x4 = []
+    for d in range(1, inner):
+        part = x_all.at[pl.ds(at, xp)]
+        x4.append(send(part, part, x_sem, xused + d - 1, near(d), col))
+
+    for copy in g3:
+        copy.wait()
+    out = pltpu.make_async_copy(g_all, gram_out, out_sem.at[0])
+    out.start()
+    for copy in x4:
+        copy.wait()
+    out2 = pltpu.make_async_copy(x_all, cross_out, out_sem.at[1])
+    out2.start()
+    out.wait()
+    out2.wait()
+
+
+def sums(panel, slab, rows, cols):
+    m, k = panel.shape
+    width = slab.shape[1]
+    inner, outer = levels(rows)
+    h = k // 2
+    split = cols if (3 * h) % (8 * inner * cols) == 0 else 1
+    piece = 3 * h // split // inner
+    xp = k // inner
+    xq = xp // outer
+    f32 = jnp.float32
+    mid_in = (max(outer - 1, 1), xq, width) if xq % 8 == 0 else (outer, xp, width)
+    g_copies = (inner - 1) + (outer - 1) + inner * (cols if split > 1 else 1) - 1
+    x_copies = 2 * (inner - 1) + 2 * (outer - 1)
+    steps = 4
+    any_space = pl.BlockSpec(memory_space=pl.ANY)
+    return pl.pallas_call(
+        functools.partial(sums_kernel, inner, outer, cols, split, 1.0 / (m * rows)),
+        out_shape=(jax.ShapeDtypeStruct((3 * h, h), f32), jax.ShapeDtypeStruct((k, width), f32)),
+        in_specs=[any_space, any_space],
+        out_specs=[any_space, any_space],
+        scratch_shapes=[
+            pltpu.VMEM((m, k), panel.dtype),
+            pltpu.VMEM((m, width), slab.dtype),
+            pltpu.VMEM((3 * h, h), f32),
+            pltpu.VMEM((max(inner - 1, 1), piece, h), f32),
+            pltpu.VMEM((outer, piece, h), f32),
+            pltpu.VMEM((3 * h, h), f32),
+            pltpu.VMEM((k, width), f32),
+            pltpu.VMEM((max(inner - 1, 1), xp, width), f32),
+            pltpu.VMEM((xp, width), f32),
+            pltpu.VMEM(mid_in, f32),
+            pltpu.VMEM((k, width), f32),
+            pltpu.SemaphoreType.DMA((2, steps)),
+            pltpu.SemaphoreType.DMA((2, g_copies)),
+            pltpu.SemaphoreType.DMA((2, x_copies)),
+            pltpu.SemaphoreType.DMA((2,)),
+        ],
+        compiler_params=pltpu.CompilerParams(collective_id=0, has_side_effects=True),
+        cost_estimate=pl.CostEstimate(flops=2 * m * k * (k + width), bytes_accessed=2 * m * (k + width), transcendentals=0),
+        name="sums",
+    )(panel, slab)
+
+
+def finish_kernel(cross_ref, invt_ref, panel_ref, slab_ref, coupling_ref, out_ref, update_ref):
+    @pl.when(pl.program_id(0) == 0)
+    def _():
+        coupling = mm(invt_ref[...], cross_ref[...])
+        coupling_ref[...] = coupling
+        update_ref[...] = mm(invt_ref[...], coupling, 0, 0).astype(jnp.bfloat16)
+
+    taken = jnp.dot(panel_ref[...], update_ref[...], preferred_element_type=jnp.float32)
+    out_ref[...] = (slab_ref[...].astype(jnp.float32) - taken).astype(jnp.bfloat16)
+
+
+def finish(cross, invt, panel, slab):
+    m, k = panel.shape
+    width = slab.shape[1]
+    rows = m // 8
+    whole = lambda i: (0, 0)
+    part = lambda i: (i, 0)
+    return pl.pallas_call(
+        finish_kernel,
+        grid=(m // rows,),
+        out_shape=(jax.ShapeDtypeStruct((k, width), jnp.float32), jax.ShapeDtypeStruct((m, width), jnp.bfloat16)),
+        in_specs=[
+            pl.BlockSpec((k, width), whole),
+            pl.BlockSpec((k, k), whole),
+            pl.BlockSpec((rows, k), part),
+            pl.BlockSpec((rows, width), part),
+        ],
+        out_specs=[pl.BlockSpec((k, width), whole), pl.BlockSpec((rows, width), part)],
+        scratch_shapes=[pltpu.VMEM((k, width), jnp.bfloat16)],
+        cost_estimate=pl.CostEstimate(flops=2 * m * k * width, bytes_accessed=2 * m * (k + 2 * width), transcendentals=0),
+        name="finish",
+    )(cross, invt, panel, slab)
 
 
 def on_device(panel, slab):
-    total_rows = panel.shape[0] * lax.axis_size("row")
-    scale = 1.0 / total_rows
-    contract = (((0,), (0,)), ((), ()))
-    gram = lax.psum(lax.dot_general(panel, panel, contract, preferred_element_type=jnp.float32) * scale, "row")
-    local_cross = lax.dot_general(panel, slab, contract, preferred_element_type=jnp.float32) * scale
-    cross = lax.psum(local_cross, "row")
+    rows, cols = lax.axis_size("row"), lax.axis_size("col")
+    gram, cross = sums(panel, slab, rows, cols)
     factor, invt = factor_and_invt(gram)
-    coupling = mm(invt, cross)
-    update = mm(invt, coupling, 0, 0).astype(jnp.bfloat16)
-    remainder = (slab.astype(jnp.float32) - jnp.dot(panel, update, preferred_element_type=jnp.float32)).astype(jnp.bfloat16)
-    share = factor.shape[1] // lax.axis_size("col")
+    coupling, remainder = finish(cross, invt, panel, slab)
+    share = factor.shape[1] // cols
     factor_part = lax.dynamic_slice_in_dim(factor, lax.axis_index("col") * share, share, 1)
     return (factor_part, coupling, remainder)
 

time: 186 us -> 78.4 us (0.42)
  waiting for transfers between devices: 108 us -> 0 us
  Pallas kernels: 34.4 us -> 75.8 us
  local copies, waits for them, and re-layouts: 15.8 us -> 1.57 us
  between operations: 14.1 us -> 0.64 us
  matrix products: 12.4 us -> 0 us
    psum x1 -> x0, waiting for transfers between devices: 108 us -> none  [on_device(): lax.psum(lax.dot_general(panel, panel, contract, preferred_element_type=j...]
    pallas_call x0 -> x2, Pallas kernels: none -> 41.5 us  [the longest x1 32.1 us: sums(): pl.pallas_call(functools.partial(sums_kernel, inner, outer, cols, split,...]
    unnamed x10 -> x0, local copies, waits for them, and re-layouts: 15.2 us -> none
    dot_general x5 -> x0, matrix products: 12.4 us -> none  [the longest x1 5.44 us: on_device(): jnp.dot(panel, update, preferred_element_type=jnp.float32)]
  transfers between devices with their start and end apart: 1 -> 0, of which waited for: 1 -> 0; matrix products, arithmetic and copies ran while one was open for 3% -> 0% of each run, Pallas kernels for 0% -> 0%
where the time goes in v1:
time: 78.4 us; the launch traced here: 78 us
  Pallas kernels  75.8 us (97%)
  local copies, waits for them, and re-layouts  1.57 us (2%)
    pallas_call x1, Pallas kernels, factor_and_invt(): pl.pallas_call(factor_kernel, out_shape=(out, out), scratch_shapes=[pltpu...  34.3 us
    pallas_call x1, Pallas kernels, sums(): pl.pallas_call(functools.partial(sums_kernel, inner, outer, cols, split,...  32.1 us
    pallas_call x1, Pallas kernels, finish(): pl.pallas_call(finish_kernel, grid=(m // rows,), out_shape=(jax.ShapeDtyp...  9.41 us

profile of v1, /device:TPU:0, one launch (start us, length us, event | category | flops | bytes accessed | tf_op | source)
XLA Modules:
  0.0 78.0 jit_solution(7280765534063244036)
XLA Ops:
  0.6 32.1 %sums.1 = (f32[384,128]{1,0:T(8,128)}, f32[256,512]{1,0:T(8,128)}) custom-call(bf16[4096,256]{1,0:T(8,128)(2,1)} %panel_ref.1, bf16[4096,512]{1,0:T(8,128)(2,1)} %slab_ref.1), custom_call_target="tpu_custom_call" | custom-call | flops 1610612736 | bytes 6291456 | tf_op jit(solution)/shard_map/sums/pallas_call | solution.py:275
  32.7 34.3 %factor.1 = (f32[256,256]{1,0:T(8,128)}, f32[256,256]{1,0:T(8,128)}) custom-call(f32[384,128]{1,0:T(8,128)} %get-tuple-element.9.gram_ref), custom_call_target="tpu_custom_call" | custom-call | flops 60000000 | bytes 786432 | tf_op jit(solution)/shard_map/factor/pallas_call | solution.py:76
  67.1 1.6 %constant_dynamic-slice_fusion = f32[256,128]{1,0:T(8,128)} fusion(f32[256,256]{1,0:T(8,128)} %get-tuple-element.10, s32[]{:T(128)S(6)} %select_n.3), kind=kLoop, calls=%fused_computation | loop fusion | bytes 262148 | tf_op jit(solution)/shard_map/dynamic_slice | solution.py:343
  68.6 9.4 %finish.1 = (f32[256,512]{1,0:T(8,128)}, bf16[4096,512]{1,0:T(8,128)(2,1)}) custom-call(f32[256,512]{1,0:T(8,128)} %get-tuple-element.11.cross_ref, f32[256,256]{1,0:T(8,128)} %get-tuple-element.12.invt_ref, bf16[4096,256]{1,0:T(8,128)(2,1)} %panel_ref.1, bf16[4096,512]{1,0:T(8,128)(2,1)} %slab_ref.1), custom_call_target="tpu_custom_call" | custom-call | flops 1073741824 | bytes 10485760 | tf_op jit(solution)/shard_map/finish/pallas_call | solution.py:320

commit v2 on v1

--- a/solution.py
+++ b/solution.py
@@ -14,72 +14,125 @@
     return lax.dot_general(a, b, (((ca,), (cb,)), ((), ())), precision=HI, preferred_element_type=jnp.float32)
 
 
-def eliminate(block, r_ref, w_ref):
-    n = block.shape[0]
-    groups = n // 8
-    lane = lax.broadcasted_iota(jnp.int32, (8, n), 1)
-    sub = lax.broadcasted_iota(jnp.int32, (8, n), 0)
-    a = [block[8 * t : 8 * t + 8, :] for t in range(groups)]
-    w = [jnp.where(lane == sub + 8 * t, 1.0, 0.0).astype(jnp.float32) for t in range(groups)]
-
-    def group(g, carry):
-        a, w = list(carry[0]), list(carry[1])
-        for j in range(8):
-            inv = lax.rsqrt(jnp.broadcast_to(a[0][j : j + 1, j : j + 1], (8, n)))
-            arow = jnp.broadcast_to(a[0][j : j + 1, :], (8, n)) * inv
-            wrow = jnp.broadcast_to(w[0][j : j + 1, :], (8, n)) * inv
-            for t in range(groups):
-                col = jnp.broadcast_to(a[t][:, j : j + 1], (8, n)) * inv
-                if t == 0:
-                    below = sub > j
-                    here = sub == j
-                    a[0], w[0] = (
-                        jnp.where(here, arow, jnp.where(below, a[0] - col * arow, a[0])),
-                        jnp.where(here, wrow, jnp.where(below, w[0] - col * wrow, w[0])),
-                    )
-                else:
-                    a[t] = a[t] - col * arow
-                    w[t] = w[t] - col * wrow
-        start = pl.multiple_of(8 * g, 8)
-        r = pltpu.roll(a[0], 8 * g, 1)
-        r_ref[pl.ds(start, 8), :] = jnp.where(lane >= sub + 8 * g, r, 0.0)
-        w_ref[pl.ds(start, 8), :] = w[0]
-        zero = jnp.zeros((8, n), jnp.float32)
-        a = [pltpu.roll(x, n - 8, 1) for x in a[1:]] + [zero]
-        w = w[1:] + [zero]
-        return tuple(a), tuple(w)
-
-    lax.fori_loop(0, groups, group, (tuple(a), tuple(w)))
-
-
-def factor_kernel(gram_ref, factor_ref, invt_ref, r_ref, w_ref):
+def row_of(x, s):
+    return jnp.broadcast_to(x[s : s + 1, :], x.shape)
+
+
+def lane_of(x, i):
+    return jnp.broadcast_to(x[:, i : i + 1], x.shape)
+
+
+def split3(x):
+    hi = x.astype(jnp.bfloat16)
+    rest = x - hi.astype(jnp.float32)
+    mid = rest.astype(jnp.bfloat16)
+    low = (rest - mid.astype(jnp.float32)).astype(jnp.bfloat16)
+    return hi, mid, low
+
+
+def outer(a, b):
+    ah, am, al = split3(a)
+    bh, bm, bl = split3(b)
+    left = jnp.concatenate([ah, ah, am, ah, al, am], axis=0)
+    right = jnp.concatenate([bh, bm, bh, bl, bh, bm], axis=0)
+    return lax.dot_general(left, right, (((0,), (0,)), ((), ())), preferred_element_type=jnp.float32)
+
+
+BLOCK, STEP, TILE = 32, 16, 128
+
+
+def eliminate(m_ref, r_ref, w_ref, b):
+    n = m_ref.shape[1]
+    groups = BLOCK // 8
+    shape = (8, TILE)
+    sub = lax.broadcasted_iota(jnp.int32, shape, 0)
+    lane = lax.broadcasted_iota(jnp.int32, shape, 1)
+    top = b * BLOCK
+    t, lo = top // TILE, top % TILE
+    tiles = n // TILE
+    inside = (lane >= lo) & (lane < lo + BLOCK)
+
+    def rows(u):
+        return [m_ref[top + 8 * g : top + 8 * g + 8, u * TILE : (u + 1) * TILE] for g in range(groups)]
+
+    own = rows(t)
+    unit = [jnp.where(inside, jnp.where(lane == sub + (lo + 8 * g), 1.0, 0.0), own[g]) for g in range(groups)]
+    other = {u: rows(u) for u in range(tiles) if u != t}
+    slabs = [own, unit] + list(other.values())
+    for first in range(0, BLOCK, STEP):
+        c = [{g: lane_of(own[g], lo + first + k) for g in range((first + k) // 8, groups)} for k in range(STEP)]
+        for k in range(STEP):
+            gj, sj = divmod(first + k, 8)
+            inv = lax.rsqrt(row_of(c[k][gj], sj))
+            l = {g: c[k][g] * inv for g in range(gj, groups)}
+            for k2 in range(k + 1, STEP):
+                g2, s2 = divmod(first + k2, 8)
+                at = row_of(l[g2], s2)
+                for g in range(g2, groups):
+                    c[k2][g] = c[k2][g] - l[g] * at
+            below = jnp.where(sub > sj, l[gj], 0.0)
+            for x in slabs:
+                pivot = row_of(x[gj], sj) * inv
+                x[gj] = jnp.where(sub == sj, pivot, x[gj] - below * pivot)
+                for g in range(gj + 1, groups):
+                    x[g] = x[g] - l[g] * pivot
+    zero = jnp.zeros(shape, jnp.float32)
+    for g in range(groups):
+        at = pl.ds(top + 8 * g, 8)
+        for u in range(tiles):
+            cols = pl.ds(u * TILE, TILE)
+            if u == t:
+                r_ref[at, cols] = jnp.where(lane >= sub + (lo + 8 * g), own[g], 0.0)
+                w_ref[at, cols] = jnp.where(lane < lo + BLOCK, unit[g], 0.0)
+            else:
+                r_ref[at, cols] = other[u][g] if u > t else zero
+                w_ref[at, cols] = other[u][g] if u < t else zero
+    end = top + BLOCK
+    if end < n:
+        done = jnp.concatenate(
+            [jnp.concatenate([unit[g] if u == t else other[u][g] for u in range(tiles)], axis=1) for g in range(groups)], axis=0
+        )
+        skip = (end // TILE) * TILE
+        taken = outer(done[:, skip:], done)
+        for u in range(tiles):
+            cols = slice(u * TILE, (u + 1) * TILE)
+            old = m_ref[end:, cols]
+            if u == t:
+                wide = lax.broadcasted_iota(jnp.int32, old.shape, 1)
+                old = jnp.where((wide >= lo) & (wide < lo + BLOCK), 0.0, old)
+            m_ref[end:, cols] = old - taken[end - skip :, cols]
+
+
+def factor_kernel(sliced, gram_ref, part_ref, invt_ref, m_ref, r_ref):
     h = gram_ref.shape[1]
-    eliminate(gram_ref[:h, :], r_ref, w_ref)
-    w1 = w_ref[...]
-    factor_ref[:h, :h] = r_ref[...]
-    invt_ref[:h, :h] = w1
-    r12 = mm(w1, gram_ref[h : 2 * h, :])
-    factor_ref[:h, h:] = r12
-    factor_ref[h:, :h] = jnp.zeros((h, h), jnp.float32)
-    invt_ref[:h, h:] = jnp.zeros((h, h), jnp.float32)
-    eliminate(gram_ref[2 * h :, :] - mm(r12, r12, 0, 0), r_ref, w_ref)
-    w2 = w_ref[...]
-    factor_ref[h:, h:] = r_ref[...]
-    invt_ref[h:, h:] = w2
-    invt_ref[h:, :h] = -mm(w2, mm(r12, w1, 0, 0))
-
-
-def factor_and_invt(blocks):
+    m_ref[:h, :h] = gram_ref[:h, :]
+    m_ref[:h, h:] = gram_ref[h : 2 * h, :]
+    m_ref[h:, h:] = gram_ref[2 * h :, :]
+    m_ref[h:, :h] = jnp.zeros((h, h), jnp.float32)
+    for b in range(m_ref.shape[0] // BLOCK):
+        eliminate(m_ref, r_ref, invt_ref, b)
+    share = part_ref.shape[1]
+    if sliced:
+        part_ref[...] = r_ref[:, pl.ds(pl.multiple_of(lax.axis_index("col") * share, TILE), share)]
+    else:
+        part_ref[...] = r_ref[...]
+
+
+def factor_and_invt(blocks, cols):
     h = blocks.shape[1]
     n = 2 * h
-    out = jax.ShapeDtypeStruct((n, n), jnp.float32)
-    return pl.pallas_call(
-        factor_kernel,
-        out_shape=(out, out),
-        scratch_shapes=[pltpu.VMEM((h, h), jnp.float32), pltpu.VMEM((h, h), jnp.float32)],
+    f32 = jnp.float32
+    sliced = (n // cols) % TILE == 0
+    part, invt = pl.pallas_call(
+        functools.partial(factor_kernel, sliced),
+        out_shape=(jax.ShapeDtypeStruct((n, n // cols if sliced else n), f32), jax.ShapeDtypeStruct((n, n), f32)),
+        scratch_shapes=[pltpu.VMEM((n, n), f32), pltpu.VMEM((n, n), f32)],
         cost_estimate=pl.CostEstimate(flops=60_000_000, bytes_accessed=3 * n * n * 4, transcendentals=n),
         name="factor",
     )(blocks)
+    if not sliced:
+        part = lax.dynamic_slice_in_dim(part, lax.axis_index("col") * (n // cols), n // cols, 1)
+    return part, invt
 
 
 def levels(rows):
@@ -337,10 +390,8 @@
 def on_device(panel, slab):
     rows, cols = lax.axis_size("row"), lax.axis_size("col")
     gram, cross = sums(panel, slab, rows, cols)
-    factor, invt = factor_and_invt(gram)
+    factor_part, invt = factor_and_invt(gram, cols)
     coupling, remainder = finish(cross, invt, panel, slab)
-    share = factor.shape[1] // cols
-    factor_part = lax.dynamic_slice_in_dim(factor, lax.axis_index("col") * share, share, 1)
     return (factor_part, coupling, remainder)
 
 

time: 78.4 us -> 50.3 us (0.64)
  Pallas kernels: 75.8 us -> 49.3 us
  local copies, waits for them, and re-layouts: 1.57 us -> 0 us
    pallas_call x1, Pallas kernels: 34.3 us -> 7.82 us  [factor_and_invt(): pl.pallas_call(functools.partial(factor_kernel, sliced), out_shape=(jax.S...]
    dynamic_slice x1 -> x0, local copies, waits for them, and re-layouts: 1.57 us -> none  [on_device(): lax.dynamic_slice_in_dim(factor, lax.axis_index('col') * share, share, 1)]
where the time goes in v2:
time: 50.3 us; the launch traced here: 50 us
  Pallas kernels  49.3 us (98%)
  between operations  0.64 us (1%)
    pallas_call x1, Pallas kernels, sums(): pl.pallas_call(functools.partial(sums_kernel, inner, outer, cols, split,...  32.1 us
    pallas_call x1, Pallas kernels, finish(): pl.pallas_call(finish_kernel, grid=(m // rows,), out_shape=(jax.ShapeDtyp...  9.41 us
    pallas_call x1, Pallas kernels, factor_and_invt(): pl.pallas_call(functools.partial(factor_kernel, sliced), out_shape=(jax.S...  7.82 us

profile of v2, /device:TPU:0, one launch (start us, length us, event | category | flops | bytes accessed | tf_op | source)
XLA Modules:
  0.0 50.0 jit_solution(5454591010316310859)
XLA Ops:
  0.6 32.1 %sums.1 = (f32[384,128]{1,0:T(8,128)}, f32[256,512]{1,0:T(8,128)}) custom-call(bf16[4096,256]{1,0:T(8,128)(2,1)} %panel_ref.1, bf16[4096,512]{1,0:T(8,128)(2,1)} %slab_ref.1), custom_call_target="tpu_custom_call" | custom-call | flops 1610612736 | bytes 6291456 | tf_op jit(solution)/shard_map/sums/pallas_call | solution.py:328
  32.7 7.8 %factor.1 = (f32[256,128]{1,0:T(8,128)}, f32[256,256]{1,0:T(8,128)}) custom-call(f32[384,128]{1,0:T(8,128)} %get-tuple-element.9.gram_ref), custom_call_target="tpu_custom_call" | custom-call | flops 60000000 | bytes 786432 | tf_op jit(solution)/shard_map/factor/pallas_call | solution.py:126
  40.6 9.4 %finish.1 = (f32[256,512]{1,0:T(8,128)}, bf16[4096,512]{1,0:T(8,128)(2,1)}) custom-call(f32[256,512]{1,0:T(8,128)} %get-tuple-element.11.cross_ref, f32[256,256]{1,0:T(8,128)} %get-tuple-element.12.invt_ref, bf16[4096,256]{1,0:T(8,128)(2,1)} %panel_ref.1, bf16[4096,512]{1,0:T(8,128)(2,1)} %slab_ref.1), custom_call_target="tpu_custom_call" | custom-call | flops 1073741824 | bytes 10485760 | tf_op jit(solution)/shard_map/finish/pallas_call | solution.py:373

commit v3 on v2

v3 whole, which is shorter than its diff:
```python
import functools

import jax
import jax.numpy as jnp
from jax import lax
from jax.experimental import pallas as pl
from jax.experimental.pallas import tpu as pltpu

HI = lax.Precision.HIGHEST
MESH = pl.DeviceIdType.MESH


def mm(a, b, ca=1, cb=0):
    return lax.dot_general(a, b, (((ca,), (cb,)), ((), ())), precision=HI, preferred_element_type=jnp.float32)


def row_of(x, s):
    return jnp.broadcast_to(x[s : s + 1, :], x.shape)


def lane_of(x, i):
    return jnp.broadcast_to(x[:, i : i + 1], x.shape)


def split3(x):
    hi = x.astype(jnp.bfloat16)
    rest = x - hi.astype(jnp.float32)
    mid = rest.astype(jnp.bfloat16)
    low = (rest - mid.astype(jnp.float32)).astype(jnp.bfloat16)
    return hi, mid, low


def outer(a, b):
    ah, am, al = split3(a)
    bh, bm, bl = split3(b)
    left = jnp.concatenate([ah, ah, am, ah, al, am], axis=0)
    right = jnp.concatenate([bh, bm, bh, bl, bh, bm], axis=0)
    return lax.dot_general(left, right, (((0,), (0,)), ((), ())), preferred_element_type=jnp.float32)


BLOCK, STEP, TILE = 32, 16, 128


def eliminate(m_ref, r_ref, w_ref, b):
    n = m_ref.shape[1]
    groups = BLOCK // 8
    shape = (8, TILE)
    sub = lax.broadcasted_iota(jnp.int32, shape, 0)
    lane = lax.broadcasted_iota(jnp.int32, shape, 1)
    top = b * BLOCK
    t, lo = top // TILE, top % TILE
    tiles = n // TILE
    inside = (lane >= lo) & (lane < lo + BLOCK)

    def rows(u):
        return [m_ref[top + 8 * g : top + 8 * g + 8, u * TILE : (u + 1) * TILE] for g in range(groups)]

    own = rows(t)
    unit = [jnp.where(inside, jnp.where(lane == sub + (lo + 8 * g), 1.0, 0.0), own[g]) for g in range(groups)]
    other = {u: rows(u) for u in range(tiles) if u != t}
    slabs = [own, unit] + list(other.values())
    for first in range(0, BLOCK, STEP):
        c = [{g: lane_of(own[g], lo + first + k) for g in range((first + k) // 8, groups)} for k in range(STEP)]
        for k in range(STEP):
            gj, sj = divmod(first + k, 8)
            inv = lax.rsqrt(row_of(c[k][gj], sj))
            l = {g: c[k][g] * inv for g in range(gj, groups)}
            for k2 in range(k + 1, STEP):
                g2, s2 = divmod(first + k2, 8)
                at = row_of(l[g2], s2)
                for g in range(g2, groups):
                    c[k2][g] = c[k2][g] - l[g] * at
            below = jnp.where(sub > sj, l[gj], 0.0)
            for x in slabs:
                pivot = row_of(x[gj], sj) * inv
                x[gj] = jnp.where(sub == sj, pivot, x[gj] - below * pivot)
                for g in range(gj + 1, groups):
                    x[g] = x[g] - l[g] * pivot
    zero = jnp.zeros(shape, jnp.float32)
    for g in range(groups):
        at = pl.ds(top + 8 * g, 8)
        for u in range(tiles):
            cols = pl.ds(u * TILE, TILE)
            if u == t:
                r_ref[at, cols] = jnp.where(lane >= sub + (lo + 8 * g), own[g], 0.0)
                w_ref[at, cols] = jnp.where(lane < lo + BLOCK, unit[g], 0.0)
            else:
                r_ref[at, cols] = other[u][g] if u > t else zero
                w_ref[at, cols] = other[u][g] if u < t else zero
    end = top + BLOCK
    if end < n:
        done = jnp.concatenate(
            [jnp.concatenate([unit[g] if u == t else other[u][g] for u in range(tiles)], axis=1) for g in range(groups)], axis=0
        )
        skip = (end // TILE) * TILE
        taken = outer(done[:, skip:], done)
        for u in range(tiles):
            cols = slice(u * TILE, (u + 1) * TILE)
            old = m_ref[end:, cols]
            if u == t:
                wide = lax.broadcasted_iota(jnp.int32, old.shape, 1)
                old = jnp.where((wide >= lo) & (wide < lo + BLOCK), 0.0, old)
            m_ref[end:, cols] = old - taken[end - skip :, cols]


def levels(rows):
    inner = 1
    while inner * inner * 4 <= rows:
        inner *= 2
    return inner, rows // inner


def send(src, dst, sems, index, to_row, to_col):
    copy = pltpu.make_async_remote_copy(
        src_ref=src, dst_ref=dst, send_sem=sems.at[0, index], recv_sem=sems.at[1, index],
        device_id={"row": to_row, "col": to_col}, device_id_type=MESH,
    )
    copy.start()
    return copy


def reduce_all(own, first_in, mid, second_in, result, sems, first, second, col):
    (na, ia, pa), (nb, ib, pb) = first, second
    ra = own.shape[0] // na
    rb = ra // nb
    used = 0

    def to(d, level, src, dst):
        nonlocal used
        used += 1
        return send(src, dst, sems, used - 1, level(d), col)

    sent = []
    for d in range(1, na):
        at = pl.multiple_of(((ia + d) % na) * ra, 8)
        sent.append(to(d, pa, own.at[pl.ds(at, ra)], first_in.at[d - 1]))
    yield
    here = pl.multiple_of(ia * ra, 8)
    total = own[pl.ds(here, ra), :]
    for d in range(1, na):
        sent[d - 1].wait()
        total = total + first_in[d - 1]
    sent = []
    if rb % 8 == 0:
        mid[...] = total
        for d in range(1, nb):
            at = pl.multiple_of(((ib + d) % nb) * rb, 8)
            sent.append(to(d, pb, mid.at[pl.ds(at, rb)], second_in.at[d - 1]))
        yield
        total = mid[pl.ds(pl.multiple_of(ib * rb, 8), rb), :]
        for d in range(1, nb):
            sent[d - 1].wait()
            total = total + second_in[d - 1]
        spot = pl.multiple_of(ia * ra + ib * rb, 8)
        result[pl.ds(spot, rb), :] = total
        sent = []
        for d in range(1, nb):
            part = result.at[pl.ds(spot, rb)]
            sent.append(to(d, pb, part, part))
        yield
        for copy in sent:
            copy.wait()
    else:
        second_in[ib] = total
        for d in range(1, nb):
            sent.append(to(d, pb, second_in.at[ib], second_in.at[ib]))
        yield
        for copy in sent:
            copy.wait()
        total = second_in[0]
        for q in range(1, nb):
            total = total + second_in[q]
        result[pl.ds(here, ra), :] = total
        yield
    sent = []
    for d in range(1, na):
        part = result.at[pl.ds(here, ra)]
        sent.append(to(d, pa, part, part))
    yield
    for copy in sent:
        copy.wait()
    yield


def reduce_scratch(k, width, na, nb):
    f32 = jnp.float32
    ra = k // na
    rb = ra // nb
    second_in = (max(nb - 1, 1), rb, width) if rb % 8 == 0 else (nb, ra, width)
    return [
        pltpu.VMEM((k, width), f32),
        pltpu.VMEM((max(na - 1, 1), ra, width), f32),
        pltpu.VMEM((ra, width), f32),
        pltpu.VMEM(second_in, f32),
        pltpu.VMEM((k, width), f32),
        pltpu.SemaphoreType.DMA((2, 2 * (na - 1) + 2 * (nb - 1))),
    ]


def product(w, x, ca):
    wh, wm, wl = split3(w)
    xh, xm, xl = split3(x)
    left = jnp.concatenate([wh, wh, wm, wh, wl, wm], axis=ca)
    right = jnp.concatenate([xh, xm, xh, xl, xh, xm], axis=0)
    return lax.dot_general(left, right, (((ca,), (0,)), ((), ())), preferred_element_type=jnp.float32)


def solve_kernel(
    inner, outer_, cols, split, scale, widths, sliced,
    panel_hbm, slab_hbm, part_out, coupling_out, update_out,
    panel, slab, g_own, g_in, g_mid, g_all, m_ref, r_ref, w_ref, part, coupling, update,
    load_sem, g_sem, out_sem, *cross_refs,
):
    row = lax.axis_index("row")
    col = lax.axis_index("col")
    high, low = row // inner, row % inner
    f32 = jnp.float32
    all_cols = range(cols if split > 1 else 1)

    def near(d):
        return high * inner + (low + d) % inner

    def far(d):
        return ((high + d) % outer_) * inner + low

    steps = load_sem.shape[1]
    chunk = panel.shape[0] // steps
    loads = []
    for which, (src, dst) in enumerate(((panel_hbm, panel), (slab_hbm, slab))):
        for t in range(steps):
            at = pl.ds(t * chunk, chunk)
            loads.append(pltpu.make_async_copy(src.at[at], dst.at[at], load_sem.at[which, t]))
    for copy in loads:
        copy.start()

    barrier = pltpu.get_barrier_semaphore()
    greeted = 0
    for d in range(inner):
        for e in all_cols:
            if d or e:
                pl.semaphore_signal(barrier, 1, device_id={"row": near(d), "col": (col + e) % cols}, device_id_type=MESH)
                greeted += 1
    for d in range(1, outer_):
        pl.semaphore_signal(barrier, 1, device_id={"row": far(d), "col": col}, device_id_type=MESH)
        greeted += 1

    def tdot(a, b):
        return lax.dot_general(a, b, (((0,), (0,)), ((), ())), preferred_element_type=f32)

    h = g_own.shape[1]
    acc = None
    for t in range(steps):
        loads[t].wait()
        p = panel[t * chunk : (t + 1) * chunk, :]
        term = tdot(p, p)
        acc = term if acc is None else acc + term
    acc = acc * scale
    g_own[:h, :] = acc[:h, :h]
    g_own[h : 2 * h, :] = acc[:h, h:]
    g_own[2 * h :, :] = acc[h:, h:]

    pl.semaphore_wait(barrier, greeted)

    share = g_own.shape[0] // split
    piece = share // inner
    base = (col * share) if split > 1 else 0
    sent = []
    for d in range(1, inner):
        at = pl.multiple_of(base + ((low + d) % inner) * piece, 8)
        sent.append(send(g_own.at[pl.ds(at, piece)], g_in.at[d - 1], g_sem, d - 1, near(d), col))
    used = inner - 1

    acc = None
    for t in range(steps):
        loads[steps + t].wait()
        term = tdot(panel[t * chunk : (t + 1) * chunk, :], slab[t * chunk : (t + 1) * chunk, :])
        acc = term if acc is None else acc + term
    acc = acc * scale
    flows = []
    left = 0
    for i, width in enumerate(widths):
        refs = cross_refs[6 * i : 6 * i + 6]
        refs[0][...] = acc[:, left : left + width]
        left += width
        ends = ((inner, low, near), (outer_, high, far))
        flows.append(reduce_all(*refs, *(ends if i == 0 else ends[::-1]), col))

    def advance():
        for flow in flows:
            next(flow)

    advance()

    mine = pl.multiple_of(base + low * piece, 8)
    total = g_own[pl.ds(mine, piece), :]
    for d in range(1, inner):
        sent[d - 1].wait()
        total = total + g_in[d - 1]
    g_mid[high] = total
    sent = []
    for d in range(1, outer_):
        sent.append(send(g_mid.at[high], g_mid.at[high], g_sem, used, far(d), col))
        used += 1
    for copy in sent:
        copy.wait()
    total = g_mid[0]
    for q in range(1, outer_):
        total = total + g_mid[q]
    g_all[pl.ds(mine, piece), :] = total
    sent = []
    for d in range(inner):
        for e in all_cols:
            if d or e:
                at = g_all.at[pl.ds(mine, piece)]
                sent.append(send(at, at, g_sem, used, near(d), (col + e) % cols))
                used += 1
    advance()
    for copy in sent:
        copy.wait()

    m_ref[:h, :h] = g_all[:h, :]
    m_ref[:h, h:] = g_all[h : 2 * h, :]
    m_ref[h:, h:] = g_all[2 * h :, :]
    m_ref[h:, :h] = jnp.zeros((h, h), f32)
    count = m_ref.shape[0] // BLOCK
    for b in range(count):
        eliminate(m_ref, r_ref, w_ref, b)
        if b in (count // 4, (5 * count) // 8 + 1):
            advance()
    width = part.shape[1]
    if sliced:
        part[...] = r_ref[:, pl.ds(pl.multiple_of(col * width, TILE), width)]
    else:
        part[...] = r_ref[...]
    out = [pltpu.make_async_copy(part, part_out, out_sem.at[0])]
    out[0].start()
    advance()

    w = w_ref[...]
    cross = jnp.concatenate([cross_refs[6 * i + 4][...] for i in range(len(widths))], axis=1)
    x = product(w, cross, 1)
    coupling[...] = x
    out.append(pltpu.make_async_copy(coupling, coupling_out, out_sem.at[1]))
    out[1].start()
    update[...] = product(w, x, 0).astype(jnp.bfloat16)
    out.append(pltpu.make_async_copy(update, update_out, out_sem.at[2]))
    out[2].start()
    for copy in out:
        copy.wait()


def solve(panel, slab, rows, cols):
    m, k = panel.shape
    width = slab.shape[1]
    inner, outer_ = levels(rows)
    h = k // 2
    split = cols if (3 * h) % (8 * inner * cols) == 0 else 1
    piece = 3 * h // split // inner
    sliced = (k // cols) % TILE == 0
    share = k // cols if sliced else k
    f32, bf16 = jnp.float32, jnp.bfloat16
    ends = ((inner, outer_), (outer_, inner))
    quarter = width // 4
    widths = (width - quarter, quarter) if quarter % TILE == 0 and k % (8 * rows) == 0 else (width,)
    steps = 4
    g_copies = (inner - 1) + (outer_ - 1) + inner * (cols if split > 1 else 1) - 1
    hbm = pl.BlockSpec(memory_space=pl.ANY)
    scratch = [
        pltpu.VMEM((m, k), bf16),
        pltpu.VMEM((m, width), bf16),
        pltpu.VMEM((3 * h, h), f32),
        pltpu.VMEM((max(inner - 1, 1), piece, h), f32),
        pltpu.VMEM((outer_, piece, h), f32),
        pltpu.VMEM((3 * h, h), f32),
        pltpu.VMEM((k, k), f32),
        pltpu.VMEM((k, k), f32),
        pltpu.VMEM((k, k), f32),
        pltpu.VMEM((k, share), f32),
        pltpu.VMEM((k, width), f32),
        pltpu.VMEM((k, width), bf16),
        pltpu.SemaphoreType.DMA((2, steps)),
        pltpu.SemaphoreType.DMA((2, g_copies)),
        pltpu.SemaphoreType.DMA((3,)),
    ]
    for i, w in enumerate(widths):
        scratch += reduce_scratch(k, w, *ends[i])
    part, coupling, update = pl.pallas_call(
        functools.partial(solve_kernel, inner, outer_, cols, split, 1.0 / (m * rows), widths, sliced),
        out_shape=(
            jax.ShapeDtypeStruct((k, share), f32),
            jax.ShapeDtypeStruct((k, width), f32),
            jax.ShapeDtypeStruct((k, width), bf16),
        ),
        in_specs=[hbm, hbm],
        out_specs=[hbm, hbm, hbm],
        scratch_shapes=scratch,
        compiler_params=pltpu.CompilerParams(collective_id=0, has_side_effects=True),
        cost_estimate=pl.CostEstimate(flops=2 * m * k * (k + width), bytes_accessed=2 * m * (k + width), transcendentals=0),
        name="solve",
    )(panel, slab)
    if not sliced:
        part = lax.dynamic_slice_in_dim(part, lax.axis_index("col") * (k // cols), k // cols, 1)
    return part, coupling, update


def finish_kernel(part_ref, coupling_ref, update_ref, panel_ref, slab_ref, part_out, coupling_out, out_ref):
    @pl.when(pl.program_id(0) == 0)
    def _():
        part_out[...] = part_ref[...]
        coupling_out[...] = coupling_ref[...]

    taken = jnp.dot(panel_ref[...], update_ref[...], preferred_element_type=jnp.float32)
    out_ref[...] = (slab_ref[...].astype(jnp.float32) - taken).astype(jnp.bfloat16)


def finish(part, coupling, update, panel, slab):
    m, k = panel.shape
    width = slab.shape[1]
    rows = m // 8
    whole = lambda i: (0, 0)
    tile = lambda i: (i, 0)
    return pl.pallas_call(
        finish_kernel,
        grid=(m // rows,),
        out_shape=(
            jax.ShapeDtypeStruct(part.shape, part.dtype),
            jax.ShapeDtypeStruct(coupling.shape, coupling.dtype),
            jax.ShapeDtypeStruct((m, width), jnp.bfloat16),
        ),
        in_specs=[
            pl.BlockSpec(part.shape, whole),
            pl.BlockSpec((k, width), whole),
            pl.BlockSpec((k, width), whole),
            pl.BlockSpec((rows, k), tile),
            pl.BlockSpec((rows, width), tile),
        ],
        out_specs=[pl.BlockSpec(part.shape, whole), pl.BlockSpec((k, width), whole), pl.BlockSpec((rows, width), tile)],
        cost_estimate=pl.CostEstimate(flops=2 * m * k * width, bytes_accessed=2 * m * (k + 2 * width), transcendentals=0),
        name="finish",
    )(part, coupling, update, panel, slab)


def on_device(panel, slab):
    rows, cols = lax.axis_size("row"), lax.axis_size("col")
    part, coupling, update = solve(panel, slab, rows, cols)
    return finish(part, coupling, update, panel, slab)


def solution(mesh):
    from jax.sharding import PartitionSpec as P

    return jax.shard_map(
        on_device,
        mesh=mesh,
        in_specs=(P("row", None), P("row", "col")),
        out_specs=(P(None, "col"), P(None, "col"), P("row", "col")),
        check_vma=False,
    )
```

time: 50.3 us -> 43.1 us (0.86)
  Pallas kernels: 49.3 us -> 42.2 us
    pallas_call x2 -> x1, Pallas kernels: 39.9 us -> 33.9 us  [solve(): pl.pallas_call(functools.partial(solve_kernel, inner, outer_, cols, split...]
    pallas_call x1, Pallas kernels: 9.41 us -> 8.31 us  [finish(): pl.pallas_call(finish_kernel, grid=(m // rows,), out_shape=(jax.ShapeDtyp...]
where the time goes in v3:
time: 43.1 us; the launch traced here: 42.8 us
  Pallas kernels  42.2 us (98%)
  between operations  0.64 us (1%)
    pallas_call x1, Pallas kernels, solve(): pl.pallas_call(functools.partial(solve_kernel, inner, outer_, cols, split...  33.9 us
    pallas_call x1, Pallas kernels, finish(): pl.pallas_call(finish_kernel, grid=(m // rows,), out_shape=(jax.ShapeDtyp...  8.31 us

profile of v3, /device:TPU:0, one launch (start us, length us, event | category | flops | bytes accessed | tf_op | source)
XLA Modules:
  0.0 42.8 jit_solution(1717192987409308496)
XLA Ops:
  0.6 33.9 %solve.1 = (f32[256,128]{1,0:T(8,128)}, f32[256,512]{1,0:T(8,128)}, bf16[256,512]{1,0:T(8,128)(2,1)}) custom-call(bf16[4096,256]{1,0:T(8,128)(2,1)} %panel_ref.1, bf16[4096,512]{1,0:T(8,128)(2,1)} %slab_ref.1), custom_call_target="tpu_custom_call" | custom-call | flops 1610612736 | bytes 6291456 | tf_op jit(solution)/shard_map/solve/pallas_call | solution.py:387
  34.5 8.3 %finish.1 = (f32[256,128]{1,0:T(8,128)}, f32[256,512]{1,0:T(8,128)}, bf16[4096,512]{1,0:T(8,128)(2,1)}) custom-call(f32[256,128]{1,0:T(8,128)} %get-tuple-element.6.part_ref, f32[256,512]{1,0:T(8,128)} %get-tuple-element.7.coupling_ref, bf16[256,512]{1,0:T(8,128)(2,1)} %get-tuple-element.8.update_ref, bf16[4096,256]{1,0:T(8,128)(2,1)} %panel_ref.1, ...), custom_call_target="tpu_custom_call" | custom-call | flops 1073741824 | bytes 10485760 | tf_op jit(solution)/shard_map/finish/pallas_call | solution.py:422

commit v4 on v3

--- a/solution.py
+++ b/solution.py
@@ -394,7 +394,7 @@
         in_specs=[hbm, hbm],
         out_specs=[hbm, hbm, hbm],
         scratch_shapes=scratch,
-        compiler_params=pltpu.CompilerParams(collective_id=0, has_side_effects=True),
+        compiler_params=pltpu.CompilerParams(collective_id=0, has_side_effects=True, vmem_limit_bytes=20 << 20),
         cost_estimate=pl.CostEstimate(flops=2 * m * k * (k + width), bytes_accessed=2 * m * (k + width), transcendentals=0),
         name="solve",
     )(panel, slab)
@@ -403,38 +403,40 @@
     return part, coupling, update
 
 
-def finish_kernel(part_ref, coupling_ref, update_ref, panel_ref, slab_ref, part_out, coupling_out, out_ref):
-    @pl.when(pl.program_id(0) == 0)
-    def _():
-        part_out[...] = part_ref[...]
-        coupling_out[...] = coupling_ref[...]
-
-    taken = jnp.dot(panel_ref[...], update_ref[...], preferred_element_type=jnp.float32)
-    out_ref[...] = (slab_ref[...].astype(jnp.float32) - taken).astype(jnp.bfloat16)
+def finish_kernel(chunks, part, coupling, update, panel, slab, part_out, coupling_out, out, kept, sems):
+    copies = [
+        pltpu.make_async_copy(coupling, coupling_out, sems.at[0]),
+        pltpu.make_async_copy(part, part_out, sems.at[1]),
+    ]
+    for copy in copies:
+        copy.start()
+    rows = panel.shape[0] // chunks
+    z = update[...]
+    for t in range(chunks):
+        at = pl.ds(t * rows, rows)
+        taken = jnp.dot(panel[at, :], z, preferred_element_type=jnp.float32)
+        kept[at, :] = (slab[at, :].astype(jnp.float32) - taken).astype(jnp.bfloat16)
+        copies.append(pltpu.make_async_copy(kept.at[at], out.at[at], sems.at[2 + t]))
+        copies[-1].start()
+    for copy in copies:
+        copy.wait()
 
 
 def finish(part, coupling, update, panel, slab):
     m, k = panel.shape
     width = slab.shape[1]
-    rows = m // 8
-    whole = lambda i: (0, 0)
-    tile = lambda i: (i, 0)
+    chunks = 8
     return pl.pallas_call(
-        finish_kernel,
-        grid=(m // rows,),
+        functools.partial(finish_kernel, chunks),
         out_shape=(
             jax.ShapeDtypeStruct(part.shape, part.dtype),
             jax.ShapeDtypeStruct(coupling.shape, coupling.dtype),
             jax.ShapeDtypeStruct((m, width), jnp.bfloat16),
         ),
-        in_specs=[
-            pl.BlockSpec(part.shape, whole),
-            pl.BlockSpec((k, width), whole),
-            pl.BlockSpec((k, width), whole),
-            pl.BlockSpec((rows, k), tile),
-            pl.BlockSpec((rows, width), tile),
-        ],
-        out_specs=[pl.BlockSpec(part.shape, whole), pl.BlockSpec((k, width), whole), pl.BlockSpec((rows, width), tile)],
+        in_specs=[pl.BlockSpec(memory_space=pltpu.VMEM)] * 5,
+        out_specs=[pl.BlockSpec(memory_space=pl.ANY)] * 3,
+        scratch_shapes=[pltpu.VMEM((m, width), jnp.bfloat16), pltpu.SemaphoreType.DMA((2 + chunks,))],
+        compiler_params=pltpu.CompilerParams(vmem_limit_bytes=12 << 20),
         cost_estimate=pl.CostEstimate(flops=2 * m * k * width, bytes_accessed=2 * m * (k + 2 * width), transcendentals=0),
         name="finish",
     )(part, coupling, update, panel, slab)
@@ -442,7 +444,8 @@
 
 def on_device(panel, slab):
     rows, cols = lax.axis_size("row"), lax.axis_size("col")
-    part, coupling, update = solve(panel, slab, rows, cols)
+    there = [pltpu.with_memory_space_constraint(x, pltpu.HBM) for x in (panel, slab)]
+    part, coupling, update = solve(*there, rows, cols)
     return finish(part, coupling, update, panel, slab)
 
 

time: 43.1 us -> 36.7 us (0.85)
  Pallas kernels: 42.2 us -> 35.9 us
    pallas_call x1, Pallas kernels: 8.31 us -> 2.39 us  [finish(): pl.pallas_call(functools.partial(finish_kernel, chunks), out_shape=(jax.S...]
where the time goes in v4:
time: 36.7 us; the launch traced here: 36.5 us
  Pallas kernels  35.9 us (98%)
  between operations  0.67 us (2%)
    pallas_call x1, Pallas kernels, solve(): pl.pallas_call(functools.partial(solve_kernel, inner, outer_, cols, split...  33.5 us
    pallas_call x1, Pallas kernels, finish(): pl.pallas_call(functools.partial(finish_kernel, chunks), out_shape=(jax.S...  2.39 us

profile of v4, /device:TPU:0, one launch (start us, length us, event | category | flops | bytes accessed | tf_op | source)
XLA Modules:
  0.0 36.5 jit_solution(6296657809316783146)
XLA Ops:
  0.6 0.0 copy-start
  0.6 0.0 copy-start.1
  0.6 33.5 %solve.1 = (f32[256,128]{1,0:T(8,128)S(1)}, f32[256,512]{1,0:T(8,128)S(1)}, bf16[256,512]{1,0:T(8,128)(2,1)S(1)}) custom-call(bf16[4096,256]{1,0:T(8,128)(2,1)} %panel.1, bf16[4096,512]{1,0:T(8,128)(2,1)} %slab.1), custom_call_target="tpu_custom_call" | custom-call | flops 1610612736 | bytes 6291456 | tf_op jit(solution)/shard_map/solve/pallas_call | solution.py:387
  34.1 0.0 copy-done
  34.1 0.0 copy-done.1
  34.1 2.4 %finish.1 = (f32[256,128]{1,0:T(8,128)}, f32[256,512]{1,0:T(8,128)}, bf16[4096,512]{1,0:T(8,128)(2,1)}) custom-call(f32[256,128]{1,0:T(8,128)S(1)} %get-tuple-element.6.part, f32[256,512]{1,0:T(8,128)S(1)} %get-tuple-element.7.coupling, bf16[256,512]{1,0:T(8,128)(2,1)S(1)} %get-tuple-element.8.update, bf16[4096,256]{1,0:T(8,128)(2,1)S(1)} %copy-done.1, ...), custom_call_target="tpu_custom_call" | custom-call | flops 1073741824 | bytes 10485760 | tf_op jit(solution)/shard_map/finish/pallas_call | solution.py:429
Async XLA Ops:
  0.6 33.5 %copy-start = (bf16[4096,512]{1,0:T(8,128)(2,1)S(1)}, bf16[4096,512]{1,0:T(8,128)(2,1)}, u32[]{:S(2)}) copy-start(bf16[4096,512]{1,0:T(8,128)(2,1)} %slab.1) | copy-start | bytes 12582916
  0.6 33.5 %copy-start.1 = (bf16[4096,256]{1,0:T(8,128)(2,1)S(1)}, bf16[4096,256]{1,0:T(8,128)(2,1)}, u32[]{:S(2)}) copy-start(bf16[4096,256]{1,0:T(8,128)(2,1)} %panel.1) | copy-start | bytes 6291460

commit v5 on v4

--- a/solution.py
+++ b/solution.py
@@ -39,6 +39,7 @@
 
 
 BLOCK, STEP, TILE = 32, 16, 128
+PANEL_STEPS, SLAB_STEPS = 2, 2
 
 
 def eliminate(m_ref, r_ref, w_ref, b):
@@ -141,7 +142,7 @@
         sent[d - 1].wait()
         total = total + first_in[d - 1]
     sent = []
-    if rb % 8 == 0:
+    if second_in.shape[0] < nb:
         mid[...] = total
         for d in range(1, nb):
             at = pl.multiple_of(((ib + d) % nb) * rb, 8)
@@ -171,7 +172,6 @@
         for q in range(1, nb):
             total = total + second_in[q]
         result[pl.ds(here, ra), :] = total
-        yield
     sent = []
     for d in range(1, na):
         part = result.at[pl.ds(here, ra)]
@@ -197,19 +197,23 @@
     ]
 
 
-def product(w, x, ca):
-    wh, wm, wl = split3(w)
-    xh, xm, xl = split3(x)
-    left = jnp.concatenate([wh, wh, wm, wh, wl, wm], axis=ca)
-    right = jnp.concatenate([xh, xm, xh, xl, xh, xm], axis=0)
-    return lax.dot_general(left, right, (((ca,), (0,)), ((), ())), preferred_element_type=jnp.float32)
+def stacked(x, axis):
+    h, m, l = split3(x)
+    return jnp.concatenate([h, m, h, l, h, m] if axis is None else [h, h, m, h, l, m], axis=axis or 0)
+
+
+def product(left, x, ca):
+    return lax.dot_general(left, stacked(x, None), (((ca,), (0,)), ((), ())), preferred_element_type=jnp.float32)
+
+
+PLAN = {'start': (0, 1, 2, 3), 'gram sent': (0, 1), 'gram last': (2, 3, 0, 1), 1: (2, 3), 2: (0, 1), 5: (2, 3)}
+FAR_FIRST = ()
 
 
 def solve_kernel(
-    inner, outer_, cols, split, scale, widths, sliced,
-    panel_hbm, slab_hbm, part_out, coupling_out, update_out,
-    panel, slab, g_own, g_in, g_mid, g_all, m_ref, r_ref, w_ref, part, coupling, update,
-    load_sem, g_sem, out_sem, *cross_refs,
+    inner, outer_, cols, split, scale, halves, count, sliced,
+    panel_hbm, slab_hbm, part, coupling, update, panel, slab,
+    g_own, g_in, g_mid, g_all, m_ref, r_ref, w_ref, panel_sem, slab_sem, g_sem, *cross_refs,
 ):
     row = lax.axis_index("row")
     col = lax.axis_index("col")
@@ -223,14 +227,14 @@
     def far(d):
         return ((high + d) % outer_) * inner + low
 
-    steps = load_sem.shape[1]
-    chunk = panel.shape[0] // steps
-    loads = []
-    for which, (src, dst) in enumerate(((panel_hbm, panel), (slab_hbm, slab))):
-        for t in range(steps):
-            at = pl.ds(t * chunk, chunk)
-            loads.append(pltpu.make_async_copy(src.at[at], dst.at[at], load_sem.at[which, t]))
-    for copy in loads:
+    def pieces(src, dst, sems):
+        rows = src.shape[0] // sems.shape[0]
+        parts = [pl.ds(t * rows, rows) for t in range(sems.shape[0])]
+        return [pltpu.make_async_copy(src.at[at], dst.at[at], sems.at[t]) for t, at in enumerate(parts)]
+
+    panel_loads = pieces(panel_hbm, panel, panel_sem)
+    slab_loads = pieces(slab_hbm, slab, slab_sem)
+    for copy in panel_loads:
         copy.start()
 
     barrier = pltpu.get_barrier_semaphore()
@@ -248,16 +252,19 @@
         return lax.dot_general(a, b, (((0,), (0,)), ((), ())), preferred_element_type=f32)
 
     h = g_own.shape[1]
-    acc = None
-    for t in range(steps):
-        loads[t].wait()
+    chunk = panel.shape[0] // len(panel_loads)
+    for t, load in enumerate(panel_loads):
+        load.wait()
+        if t < len(slab_loads):
+            slab_loads[t].start()
         p = panel[t * chunk : (t + 1) * chunk, :]
-        term = tdot(p, p)
-        acc = term if acc is None else acc + term
-    acc = acc * scale
-    g_own[:h, :] = acc[:h, :h]
-    g_own[h : 2 * h, :] = acc[:h, h:]
-    g_own[2 * h :, :] = acc[h:, h:]
+        top, low_right = tdot(p[:, :h], p), tdot(p[:, h:], p[:, h:])
+        acc = (top, low_right) if t == 0 else (acc[0] + top, acc[1] + low_right)
+    for copy in slab_loads[len(panel_loads) :]:
+        copy.start()
+    g_own[:h, :] = acc[0][:, :h] * scale
+    g_own[h : 2 * h, :] = acc[0][:, h:] * scale
+    g_own[2 * h :, :] = acc[1] * scale
 
     pl.semaphore_wait(barrier, greeted)
 
@@ -270,26 +277,28 @@
         sent.append(send(g_own.at[pl.ds(at, piece)], g_in.at[d - 1], g_sem, d - 1, near(d), col))
     used = inner - 1
 
-    acc = None
-    for t in range(steps):
-        loads[steps + t].wait()
-        term = tdot(panel[t * chunk : (t + 1) * chunk, :], slab[t * chunk : (t + 1) * chunk, :])
-        acc = term if acc is None else acc + term
+    chunk = slab.shape[0] // len(slab_loads)
+    for t, load in enumerate(slab_loads):
+        load.wait()
+        at = slice(t * chunk, (t + 1) * chunk)
+        term = tdot(panel[at, :], slab[at, :])
+        acc = term if t == 0 else acc + term
     acc = acc * scale
+    ends = ((inner, low, near), (outer_, high, far))
     flows = []
-    left = 0
-    for i, width in enumerate(widths):
+    width = slab.shape[1] // count
+    for i in range(count):
         refs = cross_refs[6 * i : 6 * i + 6]
-        refs[0][...] = acc[:, left : left + width]
-        left += width
-        ends = ((inner, low, near), (outer_, high, far))
-        flows.append(reduce_all(*refs, *(ends if i == 0 else ends[::-1]), col))
-
-    def advance():
-        for flow in flows:
-            next(flow)
-
-    advance()
+        refs[0][...] = acc[:, i * width : (i + 1) * width]
+        order = ends[::-1] if i in FAR_FIRST else ends
+        flows.append(reduce_all(*refs, *order, col))
+
+    def advance(point):
+        for i in PLAN.get(point, ()):
+            if i < count:
+                next(flows[i])
+
+    advance("start")
 
     mine = pl.multiple_of(base + low * piece, 8)
     total = g_own[pl.ds(mine, piece), :]
@@ -301,6 +310,7 @@
     for d in range(1, outer_):
         sent.append(send(g_mid.at[high], g_mid.at[high], g_sem, used, far(d), col))
         used += 1
+    advance("gram sent")
     for copy in sent:
         copy.wait()
     total = g_mid[0]
@@ -314,7 +324,8 @@
                 at = g_all.at[pl.ds(mine, piece)]
                 sent.append(send(at, at, g_sem, used, near(d), (col + e) % cols))
                 used += 1
-    advance()
+    advance("gram back")
+    advance("gram last")
     for copy in sent:
         copy.wait()
 
@@ -322,31 +333,28 @@
     m_ref[:h, h:] = g_all[h : 2 * h, :]
     m_ref[h:, h:] = g_all[2 * h :, :]
     m_ref[h:, :h] = jnp.zeros((h, h), f32)
-    count = m_ref.shape[0] // BLOCK
-    for b in range(count):
+    for b in range(m_ref.shape[0] // BLOCK):
         eliminate(m_ref, r_ref, w_ref, b)
-        if b in (count // 4, (5 * count) // 8 + 1):
-            advance()
-    width = part.shape[1]
+        advance(b)
+    share = part.shape[1]
     if sliced:
-        part[...] = r_ref[:, pl.ds(pl.multiple_of(col * width, TILE), width)]
+        part[...] = r_ref[:, pl.ds(pl.multiple_of(col * share, TILE), share)]
     else:
         part[...] = r_ref[...]
-    out = [pltpu.make_async_copy(part, part_out, out_sem.at[0])]
-    out[0].start()
-    advance()
 
     w = w_ref[...]
-    cross = jnp.concatenate([cross_refs[6 * i + 4][...] for i in range(len(widths))], axis=1)
-    x = product(w, cross, 1)
-    coupling[...] = x
-    out.append(pltpu.make_async_copy(coupling, coupling_out, out_sem.at[1]))
-    out[1].start()
-    update[...] = product(w, x, 0).astype(jnp.bfloat16)
-    out.append(pltpu.make_async_copy(update, update_out, out_sem.at[2]))
-    out[2].start()
-    for copy in out:
-        copy.wait()
+    across, down = stacked(w, 1), stacked(w, 0)
+    each = count // halves
+    half = slab.shape[1] // halves
+    for t in range(halves):
+        at = slice(t * half, (t + 1) * half)
+        for flow in flows[t * each : (t + 1) * each]:
+            for _ in flow:
+                pass
+        cross = jnp.concatenate([cross_refs[6 * i + 4][...] for i in range(t * each, (t + 1) * each)], axis=1)
+        x = product(across, cross, 1)
+        coupling[:, at] = x
+        update[:, at] = product(down, x, 0).astype(jnp.bfloat16)
 
 
 def solve(panel, slab, rows, cols):
@@ -359,15 +367,11 @@
     sliced = (k // cols) % TILE == 0
     share = k // cols if sliced else k
     f32, bf16 = jnp.float32, jnp.bfloat16
-    ends = ((inner, outer_), (outer_, inner))
-    quarter = width // 4
-    widths = (width - quarter, quarter) if quarter % TILE == 0 and k % (8 * rows) == 0 else (width,)
-    steps = 4
+    halves = 2 if width % (4 * TILE) == 0 else 1
+    count = 4 if halves == 2 and k % (8 * rows) == 0 else halves
     g_copies = (inner - 1) + (outer_ - 1) + inner * (cols if split > 1 else 1) - 1
     hbm = pl.BlockSpec(memory_space=pl.ANY)
     scratch = [
-        pltpu.VMEM((m, k), bf16),
-        pltpu.VMEM((m, width), bf16),
         pltpu.VMEM((3 * h, h), f32),
         pltpu.VMEM((max(inner - 1, 1), piece, h), f32),
         pltpu.VMEM((outer_, piece, h), f32),
@@ -375,24 +379,23 @@
         pltpu.VMEM((k, k), f32),
         pltpu.VMEM((k, k), f32),
         pltpu.VMEM((k, k), f32),
-        pltpu.VMEM((k, share), f32),
-        pltpu.VMEM((k, width), f32),
-        pltpu.VMEM((k, width), bf16),
-        pltpu.SemaphoreType.DMA((2, steps)),
+        pltpu.SemaphoreType.DMA((PANEL_STEPS,)),
+        pltpu.SemaphoreType.DMA((SLAB_STEPS,)),
         pltpu.SemaphoreType.DMA((2, g_copies)),
-        pltpu.SemaphoreType.DMA((3,)),
     ]
-    for i, w in enumerate(widths):
-        scratch += reduce_scratch(k, w, *ends[i])
-    part, coupling, update = pl.pallas_call(
-        functools.partial(solve_kernel, inner, outer_, cols, split, 1.0 / (m * rows), widths, sliced),
+    for i in range(count):
+        scratch += reduce_scratch(k, width // count, *((outer_, inner) if i in FAR_FIRST else (inner, outer_)))
+    part, coupling, update, panel, slab = pl.pallas_call(
+        functools.partial(solve_kernel, inner, outer_, cols, split, 1.0 / (m * rows), halves, count, sliced),
         out_shape=(
             jax.ShapeDtypeStruct((k, share), f32),
             jax.ShapeDtypeStruct((k, width), f32),
             jax.ShapeDtypeStruct((k, width), bf16),
+            jax.ShapeDtypeStruct((m, k), bf16),
+            jax.ShapeDtypeStruct((m, width), bf16),
         ),
         in_specs=[hbm, hbm],
-        out_specs=[hbm, hbm, hbm],
+        out_specs=[pl.BlockSpec(memory_space=pltpu.VMEM)] * 5,
         scratch_shapes=scratch,
         compiler_params=pltpu.CompilerParams(collective_id=0, has_side_effects=True, vmem_limit_bytes=20 << 20),
         cost_estimate=pl.CostEstimate(flops=2 * m * k * (k + width), bytes_accessed=2 * m * (k + width), transcendentals=0),
@@ -400,7 +403,7 @@
     )(panel, slab)
     if not sliced:
         part = lax.dynamic_slice_in_dim(part, lax.axis_index("col") * (k // cols), k // cols, 1)
-    return part, coupling, update
+    return part, coupling, update, panel, slab
 
 
 def finish_kernel(chunks, part, coupling, update, panel, slab, part_out, coupling_out, out, kept, sems):
@@ -445,7 +448,7 @@
 def on_device(panel, slab):
     rows, cols = lax.axis_size("row"), lax.axis_size("col")
     there = [pltpu.with_memory_space_constraint(x, pltpu.HBM) for x in (panel, slab)]
-    part, coupling, update = solve(*there, rows, cols)
+    part, coupling, update, panel, slab = solve(*there, rows, cols)
     return finish(part, coupling, update, panel, slab)
 
 

time: 36.7 us -> 33.7 us (0.918)
  Pallas kernels: 35.9 us -> 33 us
    pallas_call x1, Pallas kernels: 33.5 us -> 30.6 us  [solve(): pl.pallas_call(functools.partial(solve_kernel, inner, outer_, cols, split...]
where the time goes in v5:
time: 33.7 us; the launch traced here: 33.6 us
  Pallas kernels  33 us (98%)
  between operations  0.64 us (2%)
    pallas_call x1, Pallas kernels, solve(): pl.pallas_call(functools.partial(solve_kernel, inner, outer_, cols, split...  30.6 us
    pallas_call x1, Pallas kernels, finish(): pl.pallas_call(functools.partial(finish_kernel, chunks), out_shape=(jax.S...  2.39 us

profile of v5, /device:TPU:0, one launch (start us, length us, event | category | flops | bytes accessed | tf_op | source)
XLA Modules:
  0.0 33.6 jit_solution(16530943071030702110)
XLA Ops:
  0.6 30.6 %solve.1 = (f32[256,128]{1,0:T(8,128)S(1)}, f32[256,512]{1,0:T(8,128)S(1)}, bf16[256,512]{1,0:T(8,128)(2,1)S(1)}, bf16[4096,256]{1,0:T(8,128)(2,1)S(1)}, bf16[4096,512]{1,0:T(8,128)(2,1)S(1)}) custom-call(bf16[4096,256]{1,0:T(8,128)(2,1)} %panel_hbm.1, bf16[4096,512]{1,0:T(8,128)(2,1)} %slab_hbm.1), custom_call_target="tpu_custom_call" | custom-call | flops 1610612736 | bytes 6291456 | tf_op jit(solution)/shard_map/solve/pallas_call | solution.py:388
  31.2 2.4 %finish.1 = (f32[256,128]{1,0:T(8,128)}, f32[256,512]{1,0:T(8,128)}, bf16[4096,512]{1,0:T(8,128)(2,1)}) custom-call(f32[256,128]{1,0:T(8,128)S(1)} %get-tuple-element.8.part, f32[256,512]{1,0:T(8,128)S(1)} %get-tuple-element.9.coupling, bf16[256,512]{1,0:T(8,128)(2,1)S(1)} %get-tuple-element.10.update, bf16[4096,256]{1,0:T(8,128)(2,1)S(1)} %get-tuple-element.11.panel, ...), custom_call_target="tpu_custom_call" | custom-call | flops 1073741824 | bytes 10485760 | tf_op jit(solution)/shard_map/finish/pallas_call | solution.py:432

commit v6 on v5

--- a/solution.py
+++ b/solution.py
@@ -39,7 +39,7 @@
 
 
 BLOCK, STEP, TILE = 32, 16, 128
-PANEL_STEPS, SLAB_STEPS = 2, 2
+PANEL_STEPS = 2
 
 
 def eliminate(m_ref, r_ref, w_ref, b):
@@ -121,7 +121,7 @@
 
 
 def reduce_all(own, first_in, mid, second_in, result, sems, first, second, col):
-    (na, ia, pa), (nb, ib, pb) = first, second
+    (na, ia, pa, qa), (nb, ib, pb, qb) = first, second
     ra = own.shape[0] // na
     rb = ra // nb
     used = 0
@@ -132,20 +132,20 @@
         return send(src, dst, sems, used - 1, level(d), col)
 
     sent = []
-    for d in range(1, na):
-        at = pl.multiple_of(((ia + d) % na) * ra, 8)
+    for d in reversed(range(1, na)):
+        at = pl.multiple_of(qa(d) * ra, 8)
         sent.append(to(d, pa, own.at[pl.ds(at, ra)], first_in.at[d - 1]))
     yield
     here = pl.multiple_of(ia * ra, 8)
     total = own[pl.ds(here, ra), :]
     for d in range(1, na):
-        sent[d - 1].wait()
+        sent[-d].wait()
         total = total + first_in[d - 1]
     sent = []
     if second_in.shape[0] < nb:
         mid[...] = total
         for d in range(1, nb):
-            at = pl.multiple_of(((ib + d) % nb) * rb, 8)
+            at = pl.multiple_of(qb(d) * rb, 8)
             sent.append(to(d, pb, mid.at[pl.ds(at, rb)], second_in.at[d - 1]))
         yield
         total = mid[pl.ds(pl.multiple_of(ib * rb, 8), rb), :]
@@ -173,7 +173,7 @@
             total = total + second_in[q]
         result[pl.ds(here, ra), :] = total
     sent = []
-    for d in range(1, na):
+    for d in reversed(range(1, na)):
         part = result.at[pl.ds(here, ra)]
         sent.append(to(d, pa, part, part))
     yield
@@ -199,14 +199,18 @@
 
 def stacked(x, axis):
     h, m, l = split3(x)
-    return jnp.concatenate([h, m, h, l, h, m] if axis is None else [h, h, m, h, l, m], axis=axis or 0)
-
-
-def product(left, x, ca):
-    return lax.dot_general(left, stacked(x, None), (((ca,), (0,)), ((), ())), preferred_element_type=jnp.float32)
-
-
-PLAN = {'start': (0, 1, 2, 3), 'gram sent': (0, 1), 'gram last': (2, 3, 0, 1), 1: (2, 3), 2: (0, 1), 5: (2, 3)}
+    return jnp.concatenate([h, h, m, h, l, m] if axis else [h, m, h, l, h, m], axis=axis)
+
+
+def product(left, x):
+    right = stacked(x, 0)
+    mid = right.shape[0] // 2
+    return jnp.dot(left[:, :mid], right[:mid, :], preferred_element_type=jnp.float32) + jnp.dot(
+        left[:, mid:], right[mid:, :], preferred_element_type=jnp.float32
+    )
+
+
+PLAN = {('start', 0): (0, 1), ('start', 1): (2, 3), 'gram sent': (0, 1), 'gram last': (2, 3, 0, 1), 0: (2,), 1: (3, 0), 2: (1,), 4: (2, 3)}
 FAR_FIRST = ()
 
 
@@ -221,8 +225,17 @@
     f32 = jnp.float32
     all_cols = range(cols if split > 1 else 1)
 
+    def other(d):
+        at = low
+        bit = 1
+        while bit < inner:
+            if d & bit:
+                at = at + bit * (1 - 2 * ((low // bit) % 2))
+            bit *= 2
+        return at
+
     def near(d):
-        return high * inner + (low + d) % inner
+        return high * inner + other(d)
 
     def far(d):
         return ((high + d) % outer_) * inner + low
@@ -233,7 +246,9 @@
         return [pltpu.make_async_copy(src.at[at], dst.at[at], sems.at[t]) for t, at in enumerate(parts)]
 
     panel_loads = pieces(panel_hbm, panel, panel_sem)
-    slab_loads = pieces(slab_hbm, slab, slab_sem)
+    half = slab.shape[1] // halves
+    columns = [(slice(None), pl.ds(t * half, half)) for t in range(halves)]
+    slab_loads = [pltpu.make_async_copy(slab_hbm.at[at], slab.at[at], slab_sem.at[t]) for t, at in enumerate(columns)]
     for copy in panel_loads:
         copy.start()
 
@@ -272,38 +287,38 @@
     piece = share // inner
     base = (col * share) if split > 1 else 0
     sent = []
-    for d in range(1, inner):
-        at = pl.multiple_of(base + ((low + d) % inner) * piece, 8)
+    for d in reversed(range(1, inner)):
+        at = pl.multiple_of(base + other(d) * piece, 8)
         sent.append(send(g_own.at[pl.ds(at, piece)], g_in.at[d - 1], g_sem, d - 1, near(d), col))
     used = inner - 1
 
-    chunk = slab.shape[0] // len(slab_loads)
+    ends = ((inner, low, near, other), (outer_, high, far, lambda d: (high + d) % outer_))
+    flows = []
+    each = count // halves
+    width = half // each
+    mid = panel.shape[0] // 2
+
+    def advance(point):
+        for i in PLAN.get(point, ()):
+            if i < len(flows):
+                next(flows[i])
+
     for t, load in enumerate(slab_loads):
         load.wait()
-        at = slice(t * chunk, (t + 1) * chunk)
-        term = tdot(panel[at, :], slab[at, :])
-        acc = term if t == 0 else acc + term
-    acc = acc * scale
-    ends = ((inner, low, near), (outer_, high, far))
-    flows = []
-    width = slab.shape[1] // count
-    for i in range(count):
-        refs = cross_refs[6 * i : 6 * i + 6]
-        refs[0][...] = acc[:, i * width : (i + 1) * width]
-        order = ends[::-1] if i in FAR_FIRST else ends
-        flows.append(reduce_all(*refs, *order, col))
-
-    def advance(point):
-        for i in PLAN.get(point, ()):
-            if i < count:
-                next(flows[i])
-
-    advance("start")
+        at = slice(t * half, (t + 1) * half)
+        acc = tdot(panel[:mid, :], slab[:mid, at]) + tdot(panel[mid:, :], slab[mid:, at])
+        acc = acc * scale
+        for i in range(each):
+            refs = cross_refs[6 * len(flows) : 6 * len(flows) + 6]
+            refs[0][...] = acc[:, i * width : (i + 1) * width]
+            order = ends[::-1] if len(flows) in FAR_FIRST else ends
+            flows.append(reduce_all(*refs, *order, col))
+        advance(("start", t))
 
     mine = pl.multiple_of(base + low * piece, 8)
     total = g_own[pl.ds(mine, piece), :]
     for d in range(1, inner):
-        sent[d - 1].wait()
+        sent[-d].wait()
         total = total + g_in[d - 1]
     g_mid[high] = total
     sent = []
@@ -318,7 +333,7 @@
         total = total + g_mid[q]
     g_all[pl.ds(mine, piece), :] = total
     sent = []
-    for d in range(inner):
+    for d in reversed(range(inner)):
         for e in all_cols:
             if d or e:
                 at = g_all.at[pl.ds(mine, piece)]
@@ -343,18 +358,16 @@
         part[...] = r_ref[...]
 
     w = w_ref[...]
-    across, down = stacked(w, 1), stacked(w, 0)
-    each = count // halves
-    half = slab.shape[1] // halves
+    across, down = stacked(w, 1), stacked(w.T, 1)
     for t in range(halves):
         at = slice(t * half, (t + 1) * half)
         for flow in flows[t * each : (t + 1) * each]:
             for _ in flow:
                 pass
         cross = jnp.concatenate([cross_refs[6 * i + 4][...] for i in range(t * each, (t + 1) * each)], axis=1)
-        x = product(across, cross, 1)
+        x = product(across, cross)
         coupling[:, at] = x
-        update[:, at] = product(down, x, 0).astype(jnp.bfloat16)
+        update[:, at] = product(down, x).astype(jnp.bfloat16)
 
 
 def solve(panel, slab, rows, cols):
@@ -380,7 +393,7 @@
         pltpu.VMEM((k, k), f32),
         pltpu.VMEM((k, k), f32),
         pltpu.SemaphoreType.DMA((PANEL_STEPS,)),
-        pltpu.SemaphoreType.DMA((SLAB_STEPS,)),
+        pltpu.SemaphoreType.DMA((halves,)),
         pltpu.SemaphoreType.DMA((2, g_copies)),
     ]
     for i in range(count):

time: 33.7 us -> 32.6 us (0.967)
  Pallas kernels: 33 us -> 31.8 us
    pallas_call x1, Pallas kernels: 30.6 us -> 29.4 us  [solve(): pl.pallas_call(functools.partial(solve_kernel, inner, outer_, cols, split...]
where the time goes in v6:
time: 32.6 us; the launch traced here: 32.4 us
  Pallas kernels  31.8 us (98%)
  between operations  0.64 us (2%)
    pallas_call x1, Pallas kernels, solve(): pl.pallas_call(functools.partial(solve_kernel, inner, outer_, cols, split...  29.4 us
    pallas_call x1, Pallas kernels, finish(): pl.pallas_call(functools.partial(finish_kernel, chunks), out_shape=(jax.S...  2.39 us

profile of v6, /device:TPU:0, one launch (start us, length us, event | category | flops | bytes accessed | tf_op | source)
XLA Modules:
  0.0 32.4 jit_solution(4601593483678849874)
XLA Ops:
  0.6 29.4 %solve.1 = (f32[256,128]{1,0:T(8,128)S(1)}, f32[256,512]{1,0:T(8,128)S(1)}, bf16[256,512]{1,0:T(8,128)(2,1)S(1)}, bf16[4096,256]{1,0:T(8,128)(2,1)S(1)}, bf16[4096,512]{1,0:T(8,128)(2,1)S(1)}) custom-call(bf16[4096,256]{1,0:T(8,128)(2,1)} %panel_hbm.1, bf16[4096,512]{1,0:T(8,128)(2,1)} %slab_hbm.1), custom_call_target="tpu_custom_call" | custom-call | flops 1610612736 | bytes 6291456 | tf_op jit(solution)/shard_map/solve/pallas_call | solution.py:401
  30.0 2.4 %finish.1 = (f32[256,128]{1,0:T(8,128)}, f32[256,512]{1,0:T(8,128)}, bf16[4096,512]{1,0:T(8,128)(2,1)}) custom-call(f32[256,128]{1,0:T(8,128)S(1)} %get-tuple-element.8.part, f32[256,512]{1,0:T(8,128)S(1)} %get-tuple-element.9.coupling, bf16[256,512]{1,0:T(8,128)(2,1)S(1)} %get-tuple-element.10.update, bf16[4096,256]{1,0:T(8,128)(2,1)S(1)} %get-tuple-element.11.panel, ...), custom_call_target="tpu_custom_call" | custom-call | flops 1073741824 | bytes 10485760 | tf_op jit(solution)/shard_map/finish/pallas_call | solution.py:445

commit v7 on v6

--- a/solution.py
+++ b/solution.py
@@ -39,7 +39,7 @@
 
 
 BLOCK, STEP, TILE = 32, 16, 128
-PANEL_STEPS = 2
+PANEL_STEPS = 4
 
 
 def eliminate(m_ref, r_ref, w_ref, b):
@@ -210,7 +210,7 @@
     )
 
 
-PLAN = {('start', 0): (0, 1), ('start', 1): (2, 3), 'gram sent': (0, 1), 'gram last': (2, 3, 0, 1), 0: (2,), 1: (3, 0), 2: (1,), 4: (2, 3)}
+PLAN = {('start', 0): (0, 1), ('start', 1): (2, 3), 'gram sent': (0, 1), 'gram last': (2, 3, 0, 1), 0: (2,), 1: (0, 3, 1), 4: (2, 3)}
 FAR_FIRST = ()
 
 
@@ -358,16 +358,18 @@
         part[...] = r_ref[...]
 
     w = w_ref[...]
-    across, down = stacked(w, 1), stacked(w.T, 1)
+    left = jnp.concatenate([w, product(stacked(w.T, 1), w)], axis=0)
+    left = stacked(left, 1)
+    k = w.shape[0]
     for t in range(halves):
         at = slice(t * half, (t + 1) * half)
         for flow in flows[t * each : (t + 1) * each]:
             for _ in flow:
                 pass
         cross = jnp.concatenate([cross_refs[6 * i + 4][...] for i in range(t * each, (t + 1) * each)], axis=1)
-        x = product(across, cross)
-        coupling[:, at] = x
-        update[:, at] = product(down, x).astype(jnp.bfloat16)
+        x = product(left, cross)
+        coupling[:, at] = x[:k, :]
+        update[:, at] = x[k:, :].astype(jnp.bfloat16)
 
 
 def solve(panel, slab, rows, cols):
@@ -441,7 +443,7 @@
 def finish(part, coupling, update, panel, slab):
     m, k = panel.shape
     width = slab.shape[1]
-    chunks = 8
+    chunks = 16
     return pl.pallas_call(
         functools.partial(finish_kernel, chunks),
         out_shape=(

time: 32.6 us -> 32 us (0.982)
  Pallas kernels: 31.8 us -> 31.2 us
    pallas_call x1, Pallas kernels: 29.4 us -> 28.8 us  [solve(): pl.pallas_call(functools.partial(solve_kernel, inner, outer_, cols, split...]
where the time goes in v7:
time: 32 us; the launch traced here: 31.8 us
  Pallas kernels  31.2 us (98%)
  between operations  0.64 us (2%)
    pallas_call x1, Pallas kernels, solve(): pl.pallas_call(functools.partial(solve_kernel, inner, outer_, cols, split...  28.8 us
    pallas_call x1, Pallas kernels, finish(): pl.pallas_call(functools.partial(finish_kernel, chunks), out_shape=(jax.S...  2.38 us

profile of v7, /device:TPU:0, one launch (start us, length us, event | category | flops | bytes accessed | tf_op | source)
XLA Modules:
  0.0 31.8 jit_solution(7594533246510196882)
XLA Ops:
  0.6 28.8 %solve.1 = (f32[256,128]{1,0:T(8,128)S(1)}, f32[256,512]{1,0:T(8,128)S(1)}, bf16[256,512]{1,0:T(8,128)(2,1)S(1)}, bf16[4096,256]{1,0:T(8,128)(2,1)S(1)}, bf16[4096,512]{1,0:T(8,128)(2,1)S(1)}) custom-call(bf16[4096,256]{1,0:T(8,128)(2,1)} %panel_hbm.1, bf16[4096,512]{1,0:T(8,128)(2,1)} %slab_hbm.1), custom_call_target="tpu_custom_call" | custom-call | flops 1610612736 | bytes 6291456 | tf_op jit(solution)/shard_map/solve/pallas_call | solution.py:403
  29.4 2.4 %finish.1 = (f32[256,128]{1,0:T(8,128)}, f32[256,512]{1,0:T(8,128)}, bf16[4096,512]{1,0:T(8,128)(2,1)}) custom-call(f32[256,128]{1,0:T(8,128)S(1)} %get-tuple-element.8.part, f32[256,512]{1,0:T(8,128)S(1)} %get-tuple-element.9.coupling, bf16[256,512]{1,0:T(8,128)(2,1)S(1)} %get-tuple-element.10.update, bf16[4096,256]{1,0:T(8,128)(2,1)S(1)} %get-tuple-element.11.panel, ...), custom_call_target="tpu_custom_call" | custom-call | flops 1073741824 | bytes 10485760 | tf_op jit(solution)/shard_map/finish/pallas_call | solution.py:447

commit v8 on v7

--- a/solution.py
+++ b/solution.py
@@ -202,12 +202,8 @@
     return jnp.concatenate([h, h, m, h, l, m] if axis else [h, m, h, l, h, m], axis=axis)
 
 
-def product(left, x):
-    right = stacked(x, 0)
-    mid = right.shape[0] // 2
-    return jnp.dot(left[:, :mid], right[:mid, :], preferred_element_type=jnp.float32) + jnp.dot(
-        left[:, mid:], right[mid:, :], preferred_element_type=jnp.float32
-    )
+def product(left, right):
+    return jnp.dot(left, right, preferred_element_type=jnp.float32)
 
 
 PLAN = {('start', 0): (0, 1), ('start', 1): (2, 3), 'gram sent': (0, 1), 'gram last': (2, 3, 0, 1), 0: (2,), 1: (0, 3, 1), 4: (2, 3)}
@@ -358,18 +354,17 @@
         part[...] = r_ref[...]
 
     w = w_ref[...]
-    left = jnp.concatenate([w, product(stacked(w.T, 1), w)], axis=0)
-    left = stacked(left, 1)
-    k = w.shape[0]
+    both = stacked(w, 1), stacked(product(stacked(w.T, 1), stacked(w, 0)), 1)
     for t in range(halves):
         at = slice(t * half, (t + 1) * half)
         for flow in flows[t * each : (t + 1) * each]:
             for _ in flow:
                 pass
         cross = jnp.concatenate([cross_refs[6 * i + 4][...] for i in range(t * each, (t + 1) * each)], axis=1)
-        x = product(left, cross)
-        coupling[:, at] = x[:k, :]
-        update[:, at] = x[k:, :].astype(jnp.bfloat16)
+        right = stacked(cross, 0)
+        x, z = (product(left, right) for left in both)
+        coupling[:, at] = x
+        update[:, at] = z.astype(jnp.bfloat16)
 
 
 def solve(panel, slab, rows, cols):

time: 32 us -> 31.7 us (level)
  no operation moved by 1% of the time
where the time goes in v8:
time: 31.7 us; the launch traced here: 31.6 us
  Pallas kernels  30.9 us (97%)
  between operations  0.64 us (2%)
    pallas_call x1, Pallas kernels, solve(): pl.pallas_call(functools.partial(solve_kernel, inner, outer_, cols, split...  28.5 us
    pallas_call x1, Pallas kernels, finish(): pl.pallas_call(functools.partial(finish_kernel, chunks), out_shape=(jax.S...  2.38 us

profile of v8, /device:TPU:0, one launch (start us, length us, event | category | flops | bytes accessed | tf_op | source)
XLA Modules:
  0.0 31.6 jit_solution(556428746306041544)
XLA Ops:
  0.6 28.5 %solve.1 = (f32[256,128]{1,0:T(8,128)S(1)}, f32[256,512]{1,0:T(8,128)S(1)}, bf16[256,512]{1,0:T(8,128)(2,1)S(1)}, bf16[4096,256]{1,0:T(8,128)(2,1)S(1)}, bf16[4096,512]{1,0:T(8,128)(2,1)S(1)}) custom-call(bf16[4096,256]{1,0:T(8,128)(2,1)} %panel_hbm.1, bf16[4096,512]{1,0:T(8,128)(2,1)} %slab_hbm.1), custom_call_target="tpu_custom_call" | custom-call | flops 1610612736 | bytes 6291456 | tf_op jit(solution)/shard_map/solve/pallas_call | solution.py:398
  29.2 2.4 %finish.1 = (f32[256,128]{1,0:T(8,128)}, f32[256,512]{1,0:T(8,128)}, bf16[4096,512]{1,0:T(8,128)(2,1)}) custom-call(f32[256,128]{1,0:T(8,128)S(1)} %get-tuple-element.8.part, f32[256,512]{1,0:T(8,128)S(1)} %get-tuple-element.9.coupling, bf16[256,512]{1,0:T(8,128)(2,1)S(1)} %get-tuple-element.10.update, bf16[4096,256]{1,0:T(8,128)(2,1)S(1)} %get-tuple-element.11.panel, ...), custom_call_target="tpu_custom_call" | custom-call | flops 1073741824 | bytes 10485760 | tf_op jit(solution)/shard_map/finish/pallas_call | solution.py:442

commit v9 on v8

--- a/solution.py
+++ b/solution.py
@@ -266,13 +266,12 @@
     chunk = panel.shape[0] // len(panel_loads)
     for t, load in enumerate(panel_loads):
         load.wait()
-        if t < len(slab_loads):
-            slab_loads[t].start()
+        if t == 0:
+            for copy in slab_loads:
+                copy.start()
         p = panel[t * chunk : (t + 1) * chunk, :]
         top, low_right = tdot(p[:, :h], p), tdot(p[:, h:], p[:, h:])
         acc = (top, low_right) if t == 0 else (acc[0] + top, acc[1] + low_right)
-    for copy in slab_loads[len(panel_loads) :]:
-        copy.start()
     g_own[:h, :] = acc[0][:, :h] * scale
     g_own[h : 2 * h, :] = acc[0][:, h:] * scale
     g_own[2 * h :, :] = acc[1] * scale
@@ -335,6 +334,7 @@
                 at = g_all.at[pl.ds(mine, piece)]
                 sent.append(send(at, at, g_sem, used, near(d), (col + e) % cols))
                 used += 1
+    m_ref[h:, :h] = jnp.zeros((h, h), f32)
     advance("gram back")
     advance("gram last")
     for copy in sent:
@@ -343,16 +343,9 @@
     m_ref[:h, :h] = g_all[:h, :]
     m_ref[:h, h:] = g_all[h : 2 * h, :]
     m_ref[h:, h:] = g_all[2 * h :, :]
-    m_ref[h:, :h] = jnp.zeros((h, h), f32)
     for b in range(m_ref.shape[0] // BLOCK):
         eliminate(m_ref, r_ref, w_ref, b)
         advance(b)
-    share = part.shape[1]
-    if sliced:
-        part[...] = r_ref[:, pl.ds(pl.multiple_of(col * share, TILE), share)]
-    else:
-        part[...] = r_ref[...]
-
     w = w_ref[...]
     both = stacked(w, 1), stacked(product(stacked(w.T, 1), stacked(w, 0)), 1)
     for t in range(halves):
@@ -365,6 +358,12 @@
         x, z = (product(left, right) for left in both)
         coupling[:, at] = x
         update[:, at] = z.astype(jnp.bfloat16)
+        if t == 0:
+            share = part.shape[1]
+            if sliced:
+                part[...] = r_ref[:, pl.ds(pl.multiple_of(col * share, TILE), share)]
+            else:
+                part[...] = r_ref[...]
 
 
 def solve(panel, slab, rows, cols):

time: 31.7 us -> 31.7 us (level)
  no operation moved by 1% of the time
where the time goes in v9:
time: 31.7 us; the launch traced here: 31.6 us
  Pallas kernels  30.9 us (97%)
  between operations  0.64 us (2%)
    pallas_call x1, Pallas kernels, solve(): pl.pallas_call(functools.partial(solve_kernel, inner, outer_, cols, split...  28.5 us
    pallas_call x1, Pallas kernels, finish(): pl.pallas_call(functools.partial(finish_kernel, chunks), out_shape=(jax.S...  2.38 us

profile of v9, /device:TPU:0, one launch (start us, length us, event | category | flops | bytes accessed | tf_op | source)
XLA Modules:
  0.0 31.6 jit_solution(14579298314099580025)
XLA Ops:
  0.6 28.5 %solve.1 = (f32[256,128]{1,0:T(8,128)S(1)}, f32[256,512]{1,0:T(8,128)S(1)}, bf16[256,512]{1,0:T(8,128)(2,1)S(1)}, bf16[4096,256]{1,0:T(8,128)(2,1)S(1)}, bf16[4096,512]{1,0:T(8,128)(2,1)S(1)}) custom-call(bf16[4096,256]{1,0:T(8,128)(2,1)} %panel_hbm.1, bf16[4096,512]{1,0:T(8,128)(2,1)} %slab_hbm.1), custom_call_target="tpu_custom_call" | custom-call | flops 1610612736 | bytes 6291456 | tf_op jit(solution)/shard_map/solve/pallas_call | solution.py:397
  29.2 2.4 %finish.1 = (f32[256,128]{1,0:T(8,128)}, f32[256,512]{1,0:T(8,128)}, bf16[4096,512]{1,0:T(8,128)(2,1)}) custom-call(f32[256,128]{1,0:T(8,128)S(1)} %get-tuple-element.8.part, f32[256,512]{1,0:T(8,128)S(1)} %get-tuple-element.9.coupling, bf16[256,512]{1,0:T(8,128)(2,1)S(1)} %get-tuple-element.10.update, bf16[4096,256]{1,0:T(8,128)(2,1)S(1)} %get-tuple-element.11.panel, ...), custom_call_target="tpu_custom_call" | custom-call | flops 1073741824 | bytes 10485760 | tf_op jit(solution)/shard_map/finish/pallas_call | solution.py:441

commit v10 on v8

--- a/solution.py
+++ b/solution.py
@@ -203,7 +203,9 @@
 
 
 def product(left, right):
-    return jnp.dot(left, right, preferred_element_type=jnp.float32)
+    mid = left.shape[0] // 2
+    halves = (jnp.dot(part, right, preferred_element_type=jnp.float32) for part in (left[:mid, :], left[mid:, :]))
+    return jnp.concatenate(list(halves), axis=0)
 
 
 PLAN = {('start', 0): (0, 1), ('start', 1): (2, 3), 'gram sent': (0, 1), 'gram last': (2, 3, 0, 1), 0: (2,), 1: (0, 3, 1), 4: (2, 3)}

time: 31.7 us -> 31.8 us (level)
  no operation moved by 1% of the time
where the time goes in v10:
time: 31.8 us; the launch traced here: 31.6 us
  Pallas kernels  31 us (97%)
  between operations  0.64 us (2%)
    pallas_call x1, Pallas kernels, solve(): pl.pallas_call(functools.partial(solve_kernel, inner, outer_, cols, split...  28.6 us
    pallas_call x1, Pallas kernels, finish(): pl.pallas_call(functools.partial(finish_kernel, chunks), out_shape=(jax.S...  2.38 us

profile of v10, /device:TPU:0, one launch (start us, length us, event | category | flops | bytes accessed | tf_op | source)
XLA Modules:
  0.0 31.6 jit_solution(7869563425586407394)
XLA Ops:
  0.6 28.6 %solve.1 = (f32[256,128]{1,0:T(8,128)S(1)}, f32[256,512]{1,0:T(8,128)S(1)}, bf16[256,512]{1,0:T(8,128)(2,1)S(1)}, bf16[4096,256]{1,0:T(8,128)(2,1)S(1)}, bf16[4096,512]{1,0:T(8,128)(2,1)S(1)}) custom-call(bf16[4096,256]{1,0:T(8,128)(2,1)} %panel_hbm.1, bf16[4096,512]{1,0:T(8,128)(2,1)} %slab_hbm.1), custom_call_target="tpu_custom_call" | custom-call | flops 1610612736 | bytes 6291456 | tf_op jit(solution)/shard_map/solve/pallas_call | solution.py:400
  29.3 2.4 %finish.1 = (f32[256,128]{1,0:T(8,128)}, f32[256,512]{1,0:T(8,128)}, bf16[4096,512]{1,0:T(8,128)(2,1)}) custom-call(f32[256,128]{1,0:T(8,128)S(1)} %get-tuple-element.8.part, f32[256,512]{1,0:T(8,128)S(1)} %get-tuple-element.9.coupling, bf16[256,512]{1,0:T(8,128)(2,1)S(1)} %get-tuple-element.10.update, bf16[4096,256]{1,0:T(8,128)(2,1)S(1)} %get-tuple-element.11.panel, ...), custom_call_target="tpu_custom_call" | custom-call | flops 1073741824 | bytes 10485760 | tf_op jit(solution)/shard_map/finish/pallas_call | solution.py:444
